TPU v7x, 32 devices: a whole 2x2x4 slice. The times are simulated.
32 devices in a mesh: tile: 4 (over z), wide: 8 (over y, x, core).
Axes of the slice: x: 2, y: 2, z: 4, core: 2. Of those that a mesh axis runs over, the one named last changes fastest.
Arguments:
- coords: float32 [192, 2, 128], P(('tile', 'wide')), may hold values from 0 to 1, as said below
- fields: float32 [192, 4, 128], P(('tile', 'wide')), may hold values from -6 to 6
- counts: int32 [4, 8], P('tile'), may hold values from 1 to 6, as said below
- place: int32 [128], replicated, may hold values from 0 to 191, as said below
- neighbours: int32 [192, 3], P('tile'), may hold values from -1 to 127, as said below
Outputs:
- whitened: float32 [192, 4, 128], P(('tile', 'wide'))
- logdet: float32 [192], P(('tile', 'wide'))
Inputs may be any that keep to these rules, and one draw needn't show every extreme that they name: `coords`: each slot's points lie around a centre of its own; the slots of one tile have their centres in one strip of the first coordinate, tiles in order. `counts`: the live blocks of one tile number 4 times its devices; in every tile some device has 6. `place`: names every live slot exactly once. `neighbours`: entries of a live slot name distinct blocks of smaller ordinal whose slots lie in the same tile or the tile before; -1 marks an empty entry; every entry of a slot that is not live is -1.
All inputs are finite; a program needn't handle non-finite values.
Results may differ from a plain program's by a relative error of at most 0.0003.
Values sent between devices are 32-bit elements; how exact they have to be, the bound alone decides.
No kernel may reach another device: no remote copies, remote signals or barrier semaphores. Data moves between devices by JAX's collectives and lax.ppermute only.
A program may use at most 64 MiB of HBM per device.

v0:
```python
import math

import jax
import jax.numpy as jnp
from jax import lax
from jax.sharding import PartitionSpec as P

B = 128
K = 3


length_scale = 0.08
nugget = 0.25
root_three = math.sqrt(3.0)


def passed_along(shard, axis, by):
    length = lax.axis_size(axis)
    pairs = [(i, i + by) for i in range(length) if 0 <= i + by < length]
    return lax.ppermute(shard, axis, pairs)


def kernel(sites_left, sites_right):
    delta_x = sites_left[0][:, None] - sites_right[0][None, :]
    delta_y = sites_left[1][:, None] - sites_right[1][None, :]
    scaled = root_three / length_scale * jnp.sqrt(delta_x * delta_x + delta_y * delta_y)
    return (1.0 + scaled) * jnp.exp(-scaled)


def whiten(own_block, near_blocks, is_valid):
    weight_mask = jnp.repeat(is_valid.astype(jnp.float32), B)
    near_sites = jnp.transpose(near_blocks[:, :2, :], (1, 0, 2)).reshape(2, K * B)
    near_values = (
        jnp.transpose(near_blocks[:, 2:, :], (1, 0, 2)).reshape(4, K * B) * weight_mask[None, :]
    )
    cov_near = kernel(near_sites, near_sites) * weight_mask[:, None] * weight_mask[None, :]
    cov_near = cov_near + jnp.diag(nugget + 1.0 - weight_mask)
    cov_cross = kernel(own_block[:2], near_sites) * weight_mask[None, :]
    cov_own = kernel(own_block[:2], own_block[:2]) + nugget * jnp.eye(B, dtype=jnp.float32)
    chol_near = jnp.linalg.cholesky(cov_near)
    right_sides = jnp.concatenate([cov_cross.T, near_values.T], axis=1)
    solved = jax.scipy.linalg.solve_triangular(chol_near, right_sides, lower=True)
    factor = solved[:, :B]
    reduced = solved[:, B:]
    cov_cond = cov_own - jnp.dot(factor.T, factor, precision=lax.Precision.HIGHEST)
    cond_mean = jnp.dot(factor.T, reduced, precision=lax.Precision.HIGHEST)
    chol_cond = jnp.linalg.cholesky(cov_cond)
    result = jax.scipy.linalg.solve_triangular(chol_cond, own_block[2:].T - cond_mean, lower=True)
    return (result.T, 2.0 * jnp.sum(jnp.log(jnp.diagonal(chol_cond))))


def local(coords, fields, counts, place, neighbours):
    capacity = coords.shape[0]
    owner_count = lax.axis_size("wide")
    tile_index = lax.axis_index("tile")
    wide_index = lax.axis_index("wide")
    blocks = jnp.concatenate([coords, fields], axis=1)
    tile_counts = counts[0]
    tile_table = lax.all_gather(blocks, "wide", axis=0, tiled=True)
    task_rows = wide_index * capacity + jnp.arange(capacity, dtype=jnp.int32)
    listed = neighbours[task_rows]
    is_valid = listed >= 0
    source = place[jnp.maximum(listed, 0)]
    source_device = source // capacity
    source_row = source_device % owner_count * capacity + source % capacity
    from_prior = source_device // owner_count != tile_index
    wanted = jnp.where(from_prior, source_row, 0)
    arriving = passed_along(wanted, "tile", -1)
    answer = tile_table[arriving]
    prior_near = passed_along(answer, "tile", 1)
    near_blocks = jnp.where(from_prior[:, :, None, None], prior_near, tile_table[source_row])
    result, log_terms = jax.vmap(whiten)(tile_table[task_rows], near_blocks, is_valid)
    slot_number = jnp.arange(capacity, dtype=jnp.int32)
    live_mask = (slot_number < tile_counts[wide_index]).astype(jnp.float32)
    return (result * live_mask[:, None, None], log_terms * live_mask)


def solution(mesh):
    in_specs = (
        P(("tile", "wide"), None, None),
        P(("tile", "wide"), None, None),
        P("tile", None),
        P(),
        P("tile", None),
    )
    out_specs = (P(("tile", "wide"), None, None), P(("tile", "wide")))
    return jax.shard_map(local, mesh=mesh, in_specs=in_specs, out_specs=out_specs, check_vma=False)
```

profile of v0, /device:TPU:0, one launch (start us, length us, event | category | flops | bytes accessed | tf_op | source)
XLA Modules:
  0.0 731.2 jit_solution(5676750076994903524)
XLA Ops:
  0.7 0.8 copy.50
  1.5 0.6 gather_fusion.1
  2.1 0.7 gather_fusion.2
  3.1 1.3 collective-permute-start
  4.8 0.6 iota_compare_fusion.4
  5.4 0.6 iota_compare_fusion.5
  6.0 0.7 iota_compare_fusion.2
  6.7 0.5 iota_multiply_fusion
  7.3 0.7 fusion.28
  8.0 10.7 %all_gather.3 = f32[48,6,128]{2,1,0:T(8,128)S(1)} all-gather(f32[6,6,128]{2,1,0:T(8,128)S(1)} %pad_maximum_fusion.2), channel_id=1, replica_groups=mesh['tile'=4,'wide'=8] {'wide'}, dimensions={0}, use_global_device_ids=true | all-gather | bytes 165888 | tf_op jit(solution)/shard_map/all_gather | solution.py:59
  18.9 0.6 gather_fusion
  19.5 0.6 constant_dynamic-slice_fusion.1
  20.2 0.6 gather_fusion.3
  20.8 4.5 collective-permute-start.1
  25.4 1.1 compare_convert_fusion.1
  26.5 0.6 gather_fusion.4
  27.1 0.3 collective-permute-done.1
  27.5 0.6 fusion.35
  28.2 0.6 copy-done.13
  28.8 5.7 add_multiply_fusion
  34.5 1.7 copy-done.3
  36.2 71.0 %custom-call.34 = f32[6,128,128]{2,1,0:T(8,128)} custom-call(f32[6,128,128]{2,1,0:T(8,128)S(1)} %cholesky.197), custom_call_target="Cholesky" | custom-call | tf_op jit(solution)/shard_map/vmap(jit(cholesky))/cholesky | solution.py:40
  107.3 1.3 cholesky.168
  108.6 1.5 select_bitcast_fusion.2
  110.1 60.4 %custom-call.35 = f32[6,1,128,128]{2,3,1,0:T(8,128)} custom-call(f32[6,1,128,128]{3,2,1,0:T(8,128)} %select_bitcast_fusion.2), custom_call_target="InvertDiagBlocksLowerTriangular" | custom-call | tf_op jit(solution)/shard_map/vmap(jit(cholesky))/cholesky | solution.py:40
  170.5 2.1 constant_dynamic-update-slice_fusion.2
  172.6 2.0 convolution_subtract_fusion
  174.6 0.9 copy-done.2
  175.5 0.8 cholesky.201
  176.3 71.9 %custom-call.36 = f32[6,128,128]{2,1,0:T(8,128)} custom-call(f32[6,128,128]{2,1,0:T(8,128)} %cholesky.201), custom_call_target="Cholesky" | custom-call | tf_op jit(solution)/shard_map/vmap(jit(cholesky))/cholesky | solution.py:40
  248.2 1.8 select_bitcast_fusion.1
  250.0 60.4 %custom-call.37 = f32[6,1,128,128]{2,3,1,0:T(8,128)} custom-call(f32[6,1,128,128]{3,2,1,0:T(8,128)} %get-tuple-element.26), custom_call_target="InvertDiagBlocksLowerTriangular" | custom-call | tf_op jit(solution)/shard_map/vmap(jit(cholesky))/cholesky | solution.py:40
  310.4 1.6 convolution_dynamic-update-slice_fusion
  312.0 2.6 convolution_subtract_fusion.3
  314.7 71.8 %custom-call.38 = f32[6,128,128]{2,1,0:T(8,128)} custom-call(f32[6,128,128]{2,1,0:T(8,128)} %convolution_subtract_fusion.3), custom_call_target="Cholesky" | custom-call | tf_op jit(solution)/shard_map/vmap(jit(cholesky))/cholesky | solution.py:40
  386.5 1.4 select_reduce_fusion.2
  387.8 0.1 compare_reduce_fusion.1
  388.2 3.2 select_select_fusion
  391.4 11.9 %while.1 = (s32[]{:T(128)}, f32[6,384,384]{2,1,0:T(8,128)}, s32[3,2]{0,1:T(2,128)S(1)}, f32[3,6,128,128]{3,2,0,1:T(8,128)}, s32[]{:T(128)}) while((s32[]{:T(128)}, f32[6,384,384]{2,1,0:T(8,128)}, s32[3,2]{0,1:T(2,128)S(1)}, f32[3,6,128,128]{3,2,0,1:T(8,128)}, s32[]{:T(128)}) %tuple.36), condition=%wide.while_cond, body=%wide.while_body.sunk | while | flops 2 | bytes 788065 | solution.py:42
  391.7 0.5 fusion.58
  392.2 3.3 bitcast_dynamic-update-slice_fusion.2
  395.6 0.5 fusion.58
  396.2 3.3 bitcast_dynamic-update-slice_fusion.2
  399.5 0.5 fusion.58
  400.1 3.2 bitcast_dynamic-update-slice_fusion.2
  403.3 177.6 %custom-call.39 = f32[6,3,128,128]{2,3,1,0:T(8,128)S(1)} custom-call(f32[6,3,128,128]{3,2,1,0:T(8,128)} %bitcast.101), custom_call_target="InvertDiagBlocksLowerTriangular" | custom-call | tf_op jit(solution)/shard_map/vmap(jit(_solve_triangular))/triangular_solve | solution.py:42
  580.9 0.8 multiply_multiply_fusion
  581.7 0.8 fusion.16
  582.6 1.8 convolution_subtract_fusion.2
  584.4 0.8 fusion.20
  585.3 2.1 convolution_subtract_fusion.1
  587.4 0.8 fusion.18
  588.4 1.6 fusion
  590.0 1.4 fusion.4
  591.4 0.2 copy.61
  591.6 0.6 fusion.25
  592.2 70.6 %custom-call.40 = f32[6,128,128]{2,1,0:T(8,128)S(1)} custom-call(f32[6,128,128]{2,1,0:T(8,128)S(1)} %fusion.25), custom_call_target="Cholesky" | custom-call | tf_op jit(solution)/shard_map/vmap(jit(cholesky))/cholesky | solution.py:47
  662.8 0.1 compare_reduce_fusion
  662.9 0.1 select_bitcast_fusion
  663.1 4.7 copy.63
  667.8 1.8 gather_fusion.5
  669.6 1.1 compare_select_fusion.3
  670.7 58.9 %custom-call.41 = f32[6,1,128,128]{2,3,1,0:T(8,128)S(1)} custom-call(f32[6,1,128,128]{3,2,1,0:T(8,128)S(1)} %get-tuple-element.21), custom_call_target="InvertDiagBlocksLowerTriangular" | custom-call | tf_op jit(solution)/shard_map/vmap(jit(_solve_triangular))/triangular_solve | solution.py:48
  729.7 1.0 convolution_multiply_fusion
  (88 shorter events, 1.9 us)
Async XLA Ops:
  0.6 1.5 copy-start
  0.6 7.3 copy-start.18
  0.7 7.3 copy-start.17
  0.7 18.8 %copy-start.20 = (s32[1,8]{1,0:T(1,128)S(1)}, s32[1,8]{1,0:T(1,128)}, u32[]{:S(2)}) copy-start(s32[1,8]{1,0:T(1,128)} %param.7) | copy-start | bytes 100
  3.1 17.0 %collective-permute-start = (s32[6,3]{1,0:T(8,128)S(1)}, s32[6,3]{1,0:T(8,128)S(1)}, u32[]{:S(2)}, u32[]{:S(2)}) collective-permute-start(s32[6,3]{1,0:T(8,128)S(1)} %fusion.39), channel_id=1, source_target_pairs={{8,0},{16,8},{24,16},{9,1},{17,9},{25,17},{10,2},{18,10},{26,18},{... | collective-permute-start | bytes 224 | tf_op jit(solution)/shard_map/ppermute | solution.py:20
  19.5 7.1 copy-start.9
  20.8 6.6 collective-permute-start.1
  26.5 7.9 %copy-start.11 = (f32[1,6,3,128]{3,1,2,0:T(8,128)}, f32[1,6,3,128]{3,1,2,0:T(8,128)S(1)}, u32[]{:S(2)}) copy-start(f32[1,6,3,128]{3,1,2,0:T(8,128)S(1)} %copy.92) | copy-start | bytes 27652
  28.2 0.6 copy-start.13
  28.2 0.6 copy-start.15
  34.5 1.8 copy-start.3
  107.2 1.3 copy-start.1
  174.6 0.9 copy-start.2
  388.2 3.2 copy-start.21
  391.4 189.5 %copy-start.12 = (f32[1,6,3,128]{3,1,2,0:T(8,128)S(1)}, f32[1,6,3,128]{3,1,2,0:T(8,128)}, u32[]{:S(2)}) copy-start(f32[1,6,3,128]{3,1,2,0:T(8,128)} %copy-done.11) | copy-start | bytes 27652
  391.4 189.5 %copy-start.14 = (f32[6,384]{1,0:T(8,128)S(1)}, f32[6,384]{1,0:T(8,128)}, u32[]{:S(2)}) copy-start(f32[6,384]{1,0:T(8,128)} %copy-done.13) | copy-start | bytes 27652
  391.4 189.6 %copy-start.16 = (f32[6,384]{1,0:T(8,128)S(1)}, f32[6,384]{1,0:T(8,128)}, u32[]{:S(2)}) copy-start(f32[6,384]{1,0:T(8,128)} %copy-done.15) | copy-start | bytes 27652
  391.4 190.4 %copy-start.4 = (f32[6,384,4]{1,2,0:T(4,128)S(1)}, f32[6,384,4]{1,2,0:T(4,128)}, u32[]{:S(2)}) copy-start(f32[6,384,4]{1,2,0:T(4,128)} %fusion.35) | copy-start | bytes 110596
  585.2 4.7 copy-start.10
  588.2 3.3 copy-start.6
  588.2 3.3 copy-start.7
  588.3 74.4 %copy-start.8 = (pred[128,128]{1,0:T(8,128)(4,1)S(1)}, pred[128,128]{1,0:T(8,128)(4,1)}, u32[]{:S(2)}) copy-start(pred[128,128]{1,0:T(8,128)(4,1)} %iota_compare_fusion.5) | copy-start | bytes 49156
  588.3 74.6 %copy-start.5 = (pred[128,128]{1,0:T(8,128)(4,1)S(1)}, pred[128,128]{1,0:T(8,128)(4,1)}, u32[]{:S(2)}) copy-start(pred[128,128]{1,0:T(8,128)(4,1)} %iota_compare_fusion.4) | copy-start | bytes 49156
  663.1 66.6 %copy-start.19 = (f32[6]{0:T(128)S(1)}, f32[6]{0:T(128)}, u32[]{:S(2)}) copy-start(f32[6]{0:T(128)} %compare_convert_fusion.1) | copy-start | bytes 76
where the time goes:
time: 741 us; the launch traced here: 731 us
  other arithmetic  665 us (90%)
  local copies, waits for them, and re-layouts  28.9 us (4%)
  matrix products  18.8 us (3%)
  blocking collectives  10.7 us (1%)
    another operation x12, other arithmetic, whiten(): chol_near = jnp.linalg.cholesky(cov_near)  341 us
    another operation x5, other arithmetic, whiten(): jax.scipy.linalg.solve_triangular(chol_near, right_sides, lower=True)  182 us
    another operation x4, other arithmetic, whiten(): chol_cond = jnp.linalg.cholesky(cov_cond)  71.4 us
    another operation x3, other arithmetic, whiten(): jax.scipy.linalg.solve_triangular(chol_cond, own_block[2:].T - cond_mean,...  59.7 us
  transfers between devices with their start and end apart: 2, of which 1 were waited for; matrix products, arithmetic and copies ran while one was open for 1% of the time, Pallas kernels for 0%

commit v1 on v0

v1 whole, which is shorter than its diff:
```python
import math

import jax
import jax.numpy as jnp
from jax import lax
from jax.experimental import pallas as pl
from jax.experimental.pallas import tpu as pltpu
from jax.sharding import PartitionSpec as P

B = 128
K = 3
NB = K + 1
SUB = 8
PANEL = 16
GROUP = 8

length_scale = 0.08
nugget = 0.25
root_three = math.sqrt(3.0)

f32 = jnp.float32
bf16 = jnp.bfloat16


def split(a):
    high = a.astype(bf16)
    return high, (a - high.astype(f32)).astype(bf16)


def product(a, b, contract):
    def dot(x, y):
        return lax.dot_general(x, y, (contract, ((), ())), preferred_element_type=f32)

    return dot(a[0], b[0]) + (dot(a[0], b[1]) + dot(a[1], b[0]))


def column(v, at):
    return jnp.broadcast_to(v[:, at : at + 1], v.shape)


def eliminate(rows, first, lane):
    n = len(rows)
    lower = {}
    pivots = []
    inverse = []
    for g in range(0, n, GROUP):
        cols = {}
        for s in range(g, g + GROUP):
            for i in range(s, n):
                cols[i, s] = column(rows[i], first + s)
        for t in range(g, g + GROUP):
            pivot = cols[t, t]
            inv = 1.0 / pivot
            pivots.append(pivot)
            inverse.append(inv)
            lead = jnp.where(lane == first + t, 1.0 + pivot, rows[t])
            for i in range(t + 1, n):
                lower[i, t] = cols[i, t] * inv
                for u in range(t + 1, min(g + GROUP, i + 1)):
                    cols[i, u] = cols[i, u] - lower[i, t] * cols[u, t]
                rows[i] = rows[i] - lower[i, t] * lead
    inside = (lane >= first) & (lane < first + n)
    clean = []
    for t in range(n):
        row = jnp.where(inside & (lane > first + t), 0.0, rows[t])
        clean.append(jnp.where(lane == first + t, 1.0, row))
    back = [clean[t] * inverse[t] for t in range(n)]
    for t in range(n - 1, 0, -1):
        for i in range(t):
            back[i] = back[i] - lower[t, i] * back[t]
    return clean, pivots, back


def whiten_kernel(
    n_wide, slots, counts_ref, place_ref, near_ref, coords_ref, fields_ref, table_ref,
    out_ref, logdet_ref, cov, weight, sites, sites_t, rhs, swept,
):
    tile_index = lax.axis_index("tile")
    wide_index = lax.axis_index("wide")
    lane = lax.broadcasted_iota(jnp.int32, (SUB, B), 1)

    sites[...] = jnp.zeros_like(sites)
    rhs[...] = jnp.zeros_like(rhs)
    valid = {}
    for m in range(slots):
        for k in range(K):
            listed = near_ref[wide_index * slots + m, k]
            valid[m, k] = (listed >= 0).astype(f32)
            source = place_ref[jnp.maximum(listed, 0)]
            device = source // slots
            prior = (device // n_wide != tile_index).astype(jnp.int32)
            block = table_ref[device % n_wide, prior, source % slots]
            sites[pl.ds(m * SUB + k, 1), :] = block[0:1]
            sites[pl.ds(m * SUB + NB + k, 1), :] = block[1:2]
            rhs[k, m, 0:4, :] = block[2:6] * valid[m, k]
        sites[pl.ds(m * SUB + K, 1), :] = coords_ref[m, 0:1, :]
        sites[pl.ds(m * SUB + NB + K, 1), :] = coords_ref[m, 1:2, :]
        rhs[K, m, 0:4, :] = fields_ref[m]
        valid[m, K] = 1.0
    sites_t[...] = sites[...].T

    row_id = lax.broadcasted_iota(jnp.int32, (B, B), 0)
    col_id = lax.broadcasted_iota(jnp.int32, (B, B), 1)
    for m in range(slots):
        for c in range(NB):
            at = m * SUB + c
            x_row = jnp.broadcast_to(sites_t[:, at : at + 1], (B, B))
            y_row = jnp.broadcast_to(sites_t[:, at + NB : at + NB + 1], (B, B))
            for r in range(c + 1):
                dx = x_row - sites[pl.ds(m * SUB + r, 1), :]
                dy = y_row - sites[pl.ds(m * SUB + NB + r, 1), :]
                squared = dx * dx + dy * dy
                scaled = squared * (root_three / length_scale * lax.rsqrt(jnp.maximum(squared, 1e-30)))
                value = (1.0 + scaled) * jnp.exp(-scaled)
                if r < K:
                    value = value * (valid[m, c] * valid[m, r])
                if c == r:
                    value = value + jnp.where(row_id == col_id, nugget + 1.0 - valid[m, c], 0.0)
                cov[c * NB + r, m * B : (m + 1) * B, :] = value

    def block_step(r, dets):
        diag = cov.at[r * NB + r]
        for p in range(0, B, PANEL):
            rows = [diag[pl.ds(p + t, SUB, stride=B), :] for t in range(PANEL)]
            clean, pivots, back = eliminate(rows, p, lane)
            for t in range(PANEL):
                weight[pl.ds(p + t, SUB, stride=B), :] = jnp.where(
                    lane <= p + t, clean[t] * lax.rsqrt(pivots[t]), 0.0)
                dets = jnp.where(lane == p + t, pivots[t], dets)
                swept[pl.ds(t, SUB, stride=PANEL), :] = back[t]
            rest = B - p - PANEL
            if rest == 0:
                continue
            for m in range(slots):
                here = slice(m * B + p + PANEL, (m + 1) * B)
                old = diag[here, :]
                high, low = split(swept[m * PANEL : (m + 1) * PANEL, :])
                pad = lambda q: jnp.concatenate(
                    ([jnp.zeros((p, B), bf16)] if p else []) + [q, jnp.zeros((rest, B), bf16)], axis=0)
                change = product(split(old), (pad(high), pad(low)), ((1,), (0,)))
                ids = lax.broadcasted_iota(jnp.int32, old.shape, 1)
                kept = jnp.where((ids >= p) & (ids < p + PANEL), 0.0, old)
                diag[here, :] = kept - change

        for m in range(slots):
            here = slice(m * B, (m + 1) * B)
            w = split(weight[here, :])
            solved = product(split(rhs[r, m]), w, ((1,), (1,)))
            rhs[r, m] = solved
            solved = split(solved)

            def solve(c, carry):
                x = product(split(cov[c * NB + r, here, :]), w, ((1,), (1,)))
                cov[c * NB + r, here, :] = x
                rhs[c, m] = rhs[c, m] - product(solved, split(x), ((1,), (1,)))
                return carry

            lax.fori_loop(r + 1, NB, solve, 0)

            def update(c, carry):
                x = split(cov[c * NB + r, here, :])

                def one(e, inner):
                    y = split(cov[e * NB + r, here, :])
                    cov[c * NB + e, here, :] = cov[c * NB + e, here, :] - product(x, y, ((1,), (1,)))
                    return inner

                lax.fori_loop(r + 1, c + 1, one, 0)
                return carry

            lax.fori_loop(r + 1, NB, update, 0)
        return dets

    dets = lax.fori_loop(0, NB, block_step, jnp.ones((SUB, B), f32))
    total = jnp.sum(jnp.log(dets), axis=1, keepdims=True)
    live_count = counts_ref[0, wide_index]
    slot_id = lax.broadcasted_iota(jnp.int32, (SUB, 1), 0)
    logdet_ref[...] = jnp.broadcast_to(jnp.where(slot_id < live_count, total, 0.0), (SUB, B))
    for m in range(slots):
        live = (m < live_count).astype(f32)
        out_ref[m] = rhs[K, m, 0:4, :] * live


def local(coords, fields, counts, place, neighbours):
    slots = coords.shape[0]
    n_wide = lax.axis_size("wide")
    n_tile = lax.axis_size("tile")
    blocks = jnp.concatenate([coords, fields], axis=1)
    prior = lax.ppermute(blocks, "tile", [(i, i + 1) for i in range(n_tile - 1)])
    table = lax.all_gather(jnp.stack([blocks, prior]), "wide", axis=0)
    smem = pl.BlockSpec(memory_space=pltpu.SMEM)
    vmem = pl.BlockSpec(memory_space=pltpu.VMEM)
    result, logs = pl.pallas_call(
        lambda *refs: whiten_kernel(n_wide, slots, *refs),
        out_shape=(
            jax.ShapeDtypeStruct((slots, 4, B), f32),
            jax.ShapeDtypeStruct((SUB, B), f32),
        ),
        in_specs=[smem, smem, smem, vmem, vmem, vmem],
        out_specs=(vmem, vmem),
        scratch_shapes=[
            pltpu.VMEM((NB * NB, SUB * B, B), f32),
            pltpu.VMEM((SUB * B, B), f32),
            pltpu.VMEM((B, B), f32),
            pltpu.VMEM((B, B), f32),
            pltpu.VMEM((NB, slots, SUB, B), f32),
            pltpu.VMEM((SUB * PANEL, B), f32),
        ],
        compiler_params=pltpu.CompilerParams(vmem_limit_bytes=48 << 20),
    )(counts, place, neighbours, coords, fields, table)
    return result, logs[:slots, 0]


def solution(mesh):
    in_specs = (
        P(("tile", "wide"), None, None),
        P(("tile", "wide"), None, None),
        P("tile", None),
        P(),
        P("tile", None),
    )
    out_specs = (P(("tile", "wide"), None, None), P(("tile", "wide")))
    return jax.shard_map(local, mesh=mesh, in_specs=in_specs, out_specs=out_specs, check_vma=False)
```

time: 741 us -> 76.7 us (0.10); the launches traced: 731 us -> 76.4 us
  other arithmetic: 665 us -> 0.73 us
  Pallas kernels: 0 us -> 57.7 us
  local copies, waits for them, and re-layouts: 28.9 us -> 1.39 us
  matrix products: 18.8 us -> 0 us
    another operation x24 -> x2, other arithmetic: 654 us -> 0.73 us  [local(): table = lax.all_gather(jnp.stack([blocks, prior]), 'wide', axis=0)]
    pallas_call x0 -> x1, Pallas kernels: none -> 57.7 us  [local(): pl.pallas_call(lambda *refs: whiten_kernel(n_wide, slots, *refs), out_sha...]
    another operation x10 -> x0, matrix products: 15.8 us -> none  [the longest x4 8.32 us: whiten(): chol_near = jnp.linalg.cholesky(cov_near)]
    another operation x13 -> x0, local copies, waits for them, and re-layouts: 13.8 us -> none
  transfers between devices with their start and end apart: 2 -> 1, of which waited for: 1 -> 1; matrix products, arithmetic and copies ran while one was open for 1% -> 0% of each run, Pallas kernels for 0% -> 0%
where the time goes in v1:
time: 76.7 us; the launch traced here: 76.4 us
  Pallas kernels  57.7 us (75%)
  blocking collectives  9.59 us (13%)
  starting transfers between devices  4.93 us (6%)
  waiting for transfers between devices  1.4 us (2%)
  local copies, waits for them, and re-layouts  1.39 us (2%)
    pallas_call x1, Pallas kernels, local(): pl.pallas_call(lambda *refs: whiten_kernel(n_wide, slots, *refs), out_sha...  57.7 us
    all_gather x1, blocking collectives, local(): table = lax.all_gather(jnp.stack([blocks, prior]), 'wide', axis=0)  9.59 us
    ppermute x1, starting transfers between devices, local(): lax.ppermute(blocks, 'tile', [(i, i + 1) for i in range(n_tile - 1)])  4.93 us
  transfers between devices with their start and end apart: 1, of which 1 were waited for; matrix products, arithmetic and copies ran while one was open for 0% of the time, Pallas kernels for 0%

profile of v1, /device:TPU:0, one launch (start us, length us, event | category | flops | bytes accessed | tf_op | source)
XLA Modules:
  0.0 76.4 jit_solution(12257786880365368394)
XLA Ops:
  0.6 0.0 copy-start.4
  0.6 0.7 fusion
  1.4 4.9 %collective-permute-start = (f32[6,6,128]{2,1,0:T(8,128)S(1)}, f32[6,6,128]{2,1,0:T(8,128)S(1)}, u32[]{:S(2)}, u32[]{:S(2)}) collective-permute-start(f32[6,6,128]{2,1,0:T(8,128)S(1)} %get-tuple-element.7), channel_id=1, source_target_pairs={{0,8},{8,16},{16,24},{1,9},{9,17},{17,25},{2,10},{10,18},{18,26},{... | collective-permute-start | bytes 55304 | tf_op jit(solution)/shard_map/ppermute | solution.py:189
  6.3 0.0 copy-done.4
  6.3 0.1 copy.9.refs_2_
  6.4 1.4 %collective-permute-done = f32[6,6,128]{2,1,0:T(8,128)S(1)} collective-permute-done((f32[6,6,128]{2,1,0:T(8,128)S(1)}, f32[6,6,128]{2,1,0:T(8,128)S(1)}, u32[]{:S(2)}, u32[]{:S(2)}) %collective-permute-start) | collective-permute-done | bytes 18464 | tf_op jit(solution)/shard_map/ppermute | solution.py:189
  7.8 0.0 copy-start
  7.8 0.0 copy-start.1
  7.8 9.6 %all-gather = f32[16,6,6,128]{3,2,1,0:T(8,128)S(1)} all-gather(f32[2,6,6,128]{3,2,1,0:T(8,128)S(1)} %pad_maximum_fusion), channel_id=2, replica_groups=mesh['tile'=4,'wide'=8] {'wide'}, dimensions={0}, use_global_device_ids=true | all-gather | bytes 331776 | tf_op jit(solution)/shard_map/all_gather | solution.py:190
  17.4 0.0 copy-start.2
  17.4 0.0 copy-start.3
  17.4 0.0 copy-done
  17.4 0.0 copy-done.1
  17.4 0.6 copy-done.2
  18.1 0.0 copy-done.3
  18.1 57.7 %shard_map.68 = (f32[6,4,128]{2,1,0:T(4,128)}, f32[8,128]{1,0:T(8,128)S(1)}) custom-call(s32[1,8]{1,0:T(1,128)S(1)} %copy-done.2, s32[128]{0:T(128)S(1)} %copy-done.3, s32[48,3]{1,0:T(8,128)S(1)} %copy.9.refs_2_, f32[6,2,128]{2,1,0:T(2,128)S(1)} %copy-done.1, f32[6,4,128]{2,1,0:T(4,128)S(1)} %copy-done, f32[8,2,6,6,128]{4,3,2,1,0:T(8,128)S(1)} %bitcast.4), custom_call_target="tpu_custom_call" | custom-call | tf_op jit(solution)/shard_map/pallas_call | solution.py:193
  75.8 0.6 slice_reduce_fusion
  (1 shorter events, 0.0 us)
Async XLA Ops:
  0.6 5.7 %copy-start.4 = (s32[48,3]{0,1:T(4,128)S(1)}, s32[48,3]{0,1:T(4,128)}, u32[]{:S(2)}) copy-start(s32[48,3]{0,1:T(4,128)} %param.9) | copy-start | bytes 1732
  1.4 6.4 %collective-permute-start = (f32[6,6,128]{2,1,0:T(8,128)S(1)}, f32[6,6,128]{2,1,0:T(8,128)S(1)}, u32[]{:S(2)}, u32[]{:S(2)}) collective-permute-start(f32[6,6,128]{2,1,0:T(8,128)S(1)} %get-tuple-element.7), channel_id=1, source_target_pairs={{0,8},{8,16},{16,24},{1,9},{9,17},{17,25},{2,10},{10,18},{18,26},{... | collective-permute-start | bytes 55304 | tf_op jit(solution)/shard_map/ppermute | solution.py:189
  7.8 9.6 %copy-start = (f32[6,4,128]{2,1,0:T(4,128)S(1)}, f32[6,4,128]{2,1,0:T(4,128)}, u32[]{:S(2)}) copy-start(f32[6,4,128]{2,1,0:T(4,128)} %refs_4_.1) | copy-start | bytes 36868
  7.8 9.6 %copy-start.1 = (f32[6,2,128]{2,1,0:T(2,128)S(1)}, f32[6,2,128]{2,1,0:T(2,128)}, u32[]{:S(2)}) copy-start(f32[6,2,128]{2,1,0:T(2,128)} %refs_3_.1) | copy-start | bytes 18436
  17.4 0.7 copy-start.2
  17.4 0.7 copy-start.3

commit v2 on v1

--- a/solution.py
+++ b/solution.py
@@ -22,16 +22,45 @@
 bf16 = jnp.bfloat16
 
 
-def split(a):
-    high = a.astype(bf16)
-    return high, (a - high.astype(f32)).astype(bf16)
-
-
-def product(a, b, contract):
+def pieces(a):
+    first = a.astype(bf16)
+    rest = a - first.astype(f32)
+    second = rest.astype(bf16)
+    return first, second, (rest - second.astype(f32)).astype(bf16)
+
+
+def left(a):
+    first, second, third = pieces(a)
+    return jnp.concatenate([first, second], axis=1), jnp.concatenate([first, third], axis=1)
+
+
+def right_rows(b):
+    first, second, third = pieces(b)
+    main = jnp.concatenate(
+        [jnp.concatenate([first, first], axis=1), jnp.concatenate([second, second], axis=1)], axis=0)
+    return main, jnp.concatenate([third, first], axis=1)
+
+
+def right_cols(b, before, after):
+    def pad(q):
+        parts = [q]
+        if before:
+            parts.insert(0, jnp.zeros((before, B), bf16))
+        if after:
+            parts.append(jnp.zeros((after, B), bf16))
+        return jnp.concatenate(parts, axis=0)
+
+    first, second, third = (pad(q) for q in pieces(b))
+    row = jnp.concatenate([first, second], axis=1)
+    return jnp.concatenate([row, row], axis=0), jnp.concatenate([third, first], axis=0)
+
+
+def product(a, b, across):
     def dot(x, y):
-        return lax.dot_general(x, y, (contract, ((), ())), preferred_element_type=f32)
-
-    return dot(a[0], b[0]) + (dot(a[0], b[1]) + dot(a[1], b[0]))
+        return lax.dot_general(x, y, (((1,), (across,)), ((), ())), preferred_element_type=f32)
+
+    wide = dot(a[0], b[0])
+    return wide[:, :B] + (wide[:, B:] + dot(a[1], b[1]))
 
 
 def column(v, at):
@@ -116,12 +145,13 @@
                     value = value * (valid[m, c] * valid[m, r])
                 if c == r:
                     value = value + jnp.where(row_id == col_id, nugget + 1.0 - valid[m, c], 0.0)
-                cov[c * NB + r, m * B : (m + 1) * B, :] = value
+                cov[r, (m * NB + c) * B : (m * NB + c + 1) * B, :] = value
 
     def block_step(r, dets):
-        diag = cov.at[r * NB + r]
+        mine = cov.at[r]
+        start = pl.multiple_of(r * B, B)
         for p in range(0, B, PANEL):
-            rows = [diag[pl.ds(p + t, SUB, stride=B), :] for t in range(PANEL)]
+            rows = [mine[pl.ds(start + p + t, SUB, stride=NB * B), :] for t in range(PANEL)]
             clean, pivots, back = eliminate(rows, p, lane)
             for t in range(PANEL):
                 weight[pl.ds(p + t, SUB, stride=B), :] = jnp.where(
@@ -131,45 +161,34 @@
             rest = B - p - PANEL
             if rest == 0:
                 continue
+            ids = lax.broadcasted_iota(jnp.int32, (rest, B), 1)
             for m in range(slots):
-                here = slice(m * B + p + PANEL, (m + 1) * B)
-                old = diag[here, :]
-                high, low = split(swept[m * PANEL : (m + 1) * PANEL, :])
-                pad = lambda q: jnp.concatenate(
-                    ([jnp.zeros((p, B), bf16)] if p else []) + [q, jnp.zeros((rest, B), bf16)], axis=0)
-                change = product(split(old), (pad(high), pad(low)), ((1,), (0,)))
-                ids = lax.broadcasted_iota(jnp.int32, old.shape, 1)
-                kept = jnp.where((ids >= p) & (ids < p + PANEL), 0.0, old)
-                diag[here, :] = kept - change
-
+                here = pl.ds(start + m * NB * B + p + PANEL, rest)
+                old = mine[here, :]
+                change = product(left(old), right_cols(swept[m * PANEL : (m + 1) * PANEL, :], p, rest), 0)
+                mine[here, :] = jnp.where((ids >= p) & (ids < p + PANEL), 0.0, old) - change
+
+        for at in range(NB):
+            pl.when(r == at)(lambda at=at: couple(at))
+        return dets
+
+    def couple(r):
         for m in range(slots):
-            here = slice(m * B, (m + 1) * B)
-            w = split(weight[here, :])
-            solved = product(split(rhs[r, m]), w, ((1,), (1,)))
+            w = right_rows(weight[m * B : (m + 1) * B, :])
+            solved = product(left(rhs[r, m]), w, 1)
             rhs[r, m] = solved
-            solved = split(solved)
-
-            def solve(c, carry):
-                x = product(split(cov[c * NB + r, here, :]), w, ((1,), (1,)))
-                cov[c * NB + r, here, :] = x
-                rhs[c, m] = rhs[c, m] - product(solved, split(x), ((1,), (1,)))
-                return carry
-
-            lax.fori_loop(r + 1, NB, solve, 0)
-
-            def update(c, carry):
-                x = split(cov[c * NB + r, here, :])
-
-                def one(e, inner):
-                    y = split(cov[e * NB + r, here, :])
-                    cov[c * NB + e, here, :] = cov[c * NB + e, here, :] - product(x, y, ((1,), (1,)))
-                    return inner
-
-                lax.fori_loop(r + 1, c + 1, one, 0)
-                return carry
-
-            lax.fori_loop(r + 1, NB, update, 0)
-        return dets
+            if r == K:
+                continue
+            later = (NB - 1 - r) * B
+            x = product(left(cov[r, pl.ds((m * NB + r + 1) * B, later), :]), w, 1)
+            x_left = left(x)
+            z_left = left(solved)
+            for e in range(r + 1, NB):
+                skip = (e - r - 1) * B
+                y = right_rows(x[skip : skip + B])
+                here = pl.ds((m * NB + e) * B, later - skip)
+                cov[e, here, :] = cov[e, here, :] - product(tuple(q[skip:] for q in x_left), y, 1)
+                rhs[e, m] = rhs[e, m] - product(z_left, y, 1)
 
     dets = lax.fori_loop(0, NB, block_step, jnp.ones((SUB, B), f32))
     total = jnp.sum(jnp.log(dets), axis=1, keepdims=True)
@@ -199,7 +218,7 @@
         in_specs=[smem, smem, smem, vmem, vmem, vmem],
         out_specs=(vmem, vmem),
         scratch_shapes=[
-            pltpu.VMEM((NB * NB, SUB * B, B), f32),
+            pltpu.VMEM((NB, SUB * NB * B, B), f32),
             pltpu.VMEM((SUB * B, B), f32),
             pltpu.VMEM((B, B), f32),
             pltpu.VMEM((B, B), f32),

time: 76.7 us -> 55.1 us (0.72)
  Pallas kernels: 57.7 us -> 36.2 us
    pallas_call x1, Pallas kernels: 57.7 us -> 36.2 us  [local(): pl.pallas_call(lambda *refs: whiten_kernel(n_wide, slots, *refs), out_sha...]
where the time goes in v2:
time: 55.1 us; the launch traced here: 54.9 us
  Pallas kernels  36.2 us (66%)
  blocking collectives  9.59 us (17%)
  starting transfers between devices  4.93 us (9%)
  waiting for transfers between devices  1.4 us (3%)
  local copies, waits for them, and re-layouts  1.39 us (3%)
  other arithmetic  0.73 us (1%)
  between operations  0.68 us (1%)
    pallas_call x1, Pallas kernels, local(): pl.pallas_call(lambda *refs: whiten_kernel(n_wide, slots, *refs), out_sha...  36.2 us
    all_gather x1, blocking collectives, local(): table = lax.all_gather(jnp.stack([blocks, prior]), 'wide', axis=0)  9.59 us
    ppermute x1, starting transfers between devices, local(): lax.ppermute(blocks, 'tile', [(i, i + 1) for i in range(n_tile - 1)])  4.93 us
    ppermute x1, waiting for transfers between devices, local(): lax.ppermute(blocks, 'tile', [(i, i + 1) for i in range(n_tile - 1)])  1.4 us
  transfers between devices with their start and end apart: 1, of which 1 were waited for; matrix products, arithmetic and copies ran while one was open for 0% of the time, Pallas kernels for 0%

profile of v2, /device:TPU:0, one launch (start us, length us, event | category | flops | bytes accessed | tf_op | source)
XLA Modules:
  0.0 54.9 jit_solution(15077105023669104165)
XLA Ops:
  0.6 0.0 copy-start.4
  0.6 0.7 %fusion = (f32[1,6,6,128]{3,2,1,0:T(8,128)S(1)}, f32[6,6,128]{2,1,0:T(8,128)S(1)}) fusion(f32[6,4,128]{2,1,0:T(4,128)} %refs_4_.1, f32[6,2,128]{2,1,0:T(2,128)} %refs_3_.1), kind=kLoop, calls=%fused_computation.3 | loop fusion | flops 4608 | bytes 55296 | tf_op jit(solution)/shard_map/stack | solution.py:209
  1.4 4.9 %collective-permute-start = (f32[6,6,128]{2,1,0:T(8,128)S(1)}, f32[6,6,128]{2,1,0:T(8,128)S(1)}, u32[]{:S(2)}, u32[]{:S(2)}) collective-permute-start(f32[6,6,128]{2,1,0:T(8,128)S(1)} %get-tuple-element.7), channel_id=1, source_target_pairs={{0,8},{8,16},{16,24},{1,9},{9,17},{17,25},{2,10},{10,18},{18,26},{... | collective-permute-start | bytes 55304 | tf_op jit(solution)/shard_map/ppermute | solution.py:208
  6.3 0.0 copy-done.4
  6.3 0.1 copy.9.refs_2_
  6.4 1.4 %collective-permute-done = f32[6,6,128]{2,1,0:T(8,128)S(1)} collective-permute-done((f32[6,6,128]{2,1,0:T(8,128)S(1)}, f32[6,6,128]{2,1,0:T(8,128)S(1)}, u32[]{:S(2)}, u32[]{:S(2)}) %collective-permute-start) | collective-permute-done | bytes 18464 | tf_op jit(solution)/shard_map/ppermute | solution.py:208
  7.8 0.0 copy-start
  7.8 0.0 copy-start.1
  7.8 9.6 %all-gather = f32[16,6,6,128]{3,2,1,0:T(8,128)S(1)} all-gather(f32[2,6,6,128]{3,2,1,0:T(8,128)S(1)} %pad_maximum_fusion), channel_id=2, replica_groups=mesh['tile'=4,'wide'=8] {'wide'}, dimensions={0}, use_global_device_ids=true | all-gather | bytes 331776 | tf_op jit(solution)/shard_map/all_gather | solution.py:209
  17.4 0.0 copy-start.2
  17.4 0.0 copy-start.3
  17.4 0.0 copy-done
  17.4 0.0 copy-done.1
  17.4 0.6 %copy-done.2 = s32[1,8]{1,0:T(1,128)S(1)} copy-done((s32[1,8]{1,0:T(1,128)S(1)}, s32[1,8]{1,0:T(1,128)}, u32[]{:S(2)}) %copy-start.2) | copy-done | bytes 56
  18.1 0.0 copy-done.3
  18.1 36.2 %shard_map.68 = (f32[6,4,128]{2,1,0:T(4,128)}, f32[8,128]{1,0:T(8,128)S(1)}) custom-call(s32[1,8]{1,0:T(1,128)S(1)} %copy-done.2, s32[128]{0:T(128)S(1)} %copy-done.3, s32[48,3]{1,0:T(8,128)S(1)} %copy.9.refs_2_, f32[6,2,128]{2,1,0:T(2,128)S(1)} %copy-done.1, f32[6,4,128]{2,1,0:T(4,128)S(1)} %copy-done, f32[8,2,6,6,128]{4,3,2,1,0:T(8,128)S(1)} %bitcast.4), custom_call_target="tpu_custom_call" | custom-call | tf_op jit(solution)/shard_map/pallas_call | solution.py:212
  54.3 0.6 %slice_reduce_fusion = f32[6]{0:T(128)} fusion(f32[8,128]{1,0:T(8,128)S(1)} %get-tuple-element.5), kind=kLoop, calls=%fused_computation.2 | loop fusion | bytes 48 | tf_op jit(solution)/shard_map/slice | solution.py:230
  (1 shorter events, 0.0 us)
Async XLA Ops:
  0.6 5.7 %copy-start.4 = (s32[48,3]{0,1:T(4,128)S(1)}, s32[48,3]{0,1:T(4,128)}, u32[]{:S(2)}) copy-start(s32[48,3]{0,1:T(4,128)} %param.9) | copy-start | bytes 1732
  1.4 6.4 %collective-permute-start = (f32[6,6,128]{2,1,0:T(8,128)S(1)}, f32[6,6,128]{2,1,0:T(8,128)S(1)}, u32[]{:S(2)}, u32[]{:S(2)}) collective-permute-start(f32[6,6,128]{2,1,0:T(8,128)S(1)} %get-tuple-element.7), channel_id=1, source_target_pairs={{0,8},{8,16},{16,24},{1,9},{9,17},{17,25},{2,10},{10,18},{18,26},{... | collective-permute-start | bytes 55304 | tf_op jit(solution)/shard_map/ppermute | solution.py:208
  7.8 9.6 %copy-start = (f32[6,4,128]{2,1,0:T(4,128)S(1)}, f32[6,4,128]{2,1,0:T(4,128)}, u32[]{:S(2)}) copy-start(f32[6,4,128]{2,1,0:T(4,128)} %refs_4_.1) | copy-start | bytes 36868
  7.8 9.6 %copy-start.1 = (f32[6,2,128]{2,1,0:T(2,128)S(1)}, f32[6,2,128]{2,1,0:T(2,128)}, u32[]{:S(2)}) copy-start(f32[6,2,128]{2,1,0:T(2,128)} %refs_3_.1) | copy-start | bytes 18436
  17.4 0.7 %copy-start.2 = (s32[1,8]{1,0:T(1,128)S(1)}, s32[1,8]{1,0:T(1,128)}, u32[]{:S(2)}) copy-start(s32[1,8]{1,0:T(1,128)} %refs_0_.1) | copy-start | bytes 100
  17.4 0.7 %copy-start.3 = (s32[128]{0:T(128)S(1)}, s32[128]{0:T(128)}, u32[]{:S(2)}) copy-start(s32[128]{0:T(128)} %refs_1_.1) | copy-start | bytes 1540

commit v3 on v2

--- a/solution.py
+++ b/solution.py
@@ -41,68 +41,69 @@
     return main, jnp.concatenate([third, first], axis=1)
 
 
-def right_cols(b, before, after):
-    def pad(q):
-        parts = [q]
-        if before:
-            parts.insert(0, jnp.zeros((before, B), bf16))
-        if after:
-            parts.append(jnp.zeros((after, B), bf16))
-        return jnp.concatenate(parts, axis=0)
-
-    first, second, third = (pad(q) for q in pieces(b))
-    row = jnp.concatenate([first, second], axis=1)
-    return jnp.concatenate([row, row], axis=0), jnp.concatenate([third, first], axis=0)
-
-
-def product(a, b, across):
+def swap_sweep(panel, swept):
+    a, b, c = pieces(panel)
+    x, y, z = pieces(swept)
+    return jnp.concatenate([a, a, b, b, a, c], axis=0).T, jnp.concatenate([x, y, x, y, z, x], axis=0)
+
+
+def product(a, b):
     def dot(x, y):
-        return lax.dot_general(x, y, (((1,), (across,)), ((), ())), preferred_element_type=f32)
+        return lax.dot_general(x, y, (((1,), (1,)), ((), ())), preferred_element_type=f32)
 
     wide = dot(a[0], b[0])
     return wide[:, :B] + (wide[:, B:] + dot(a[1], b[1]))
 
 
+def left_short(a):
+    first = a.astype(bf16)
+    return jnp.concatenate([first, (a - first.astype(f32)).astype(bf16)], axis=1)
+
+
+def right_short(x):
+    first = x[:, :B]
+    return jnp.concatenate(
+        [jnp.concatenate([first, first], axis=1),
+         jnp.concatenate([x[:, B:], jnp.zeros_like(first)], axis=1)], axis=0)
+
+
+def product_short(a, b):
+    wide = lax.dot_general(a, b, (((1,), (1,)), ((), ())), preferred_element_type=f32)
+    return wide[:, :B] + wide[:, B:]
+
+
 def column(v, at):
     return jnp.broadcast_to(v[:, at : at + 1], v.shape)
 
 
 def eliminate(rows, first, lane):
     n = len(rows)
-    lower = {}
     pivots = []
-    inverse = []
+    scaled = []
     for g in range(0, n, GROUP):
+        end = g + GROUP
         cols = {}
-        for s in range(g, g + GROUP):
+        for s in range(g, end):
             for i in range(s, n):
                 cols[i, s] = column(rows[i], first + s)
-        for t in range(g, g + GROUP):
+        for t in range(g, end):
             pivot = cols[t, t]
             inv = 1.0 / pivot
             pivots.append(pivot)
-            inverse.append(inv)
-            lead = jnp.where(lane == first + t, 1.0 + pivot, rows[t])
-            for i in range(t + 1, n):
-                lower[i, t] = cols[i, t] * inv
-                for u in range(t + 1, min(g + GROUP, i + 1)):
-                    cols[i, u] = cols[i, u] - lower[i, t] * cols[u, t]
-                rows[i] = rows[i] - lower[i, t] * lead
-    inside = (lane >= first) & (lane < first + n)
-    clean = []
-    for t in range(n):
-        row = jnp.where(inside & (lane > first + t), 0.0, rows[t])
-        clean.append(jnp.where(lane == first + t, 1.0, row))
-    back = [clean[t] * inverse[t] for t in range(n)]
-    for t in range(n - 1, 0, -1):
-        for i in range(t):
-            back[i] = back[i] - lower[t, i] * back[t]
-    return clean, pivots, back
+            scaled.append(jnp.where(lane == first + t, 1.0 + pivot, rows[t]) * inv)
+            for u in range(t + 1, end):
+                lower = cols[u, t] * inv
+                for i in range(u, n):
+                    cols[i, u] = cols[i, u] - cols[i, t] * lower
+                rows[u] = rows[u] - cols[u, t] * scaled[t]
+            for i in range(end, n):
+                rows[i] = rows[i] - cols[i, t] * scaled[t]
+    return pivots, scaled
 
 
 def whiten_kernel(
     n_wide, slots, counts_ref, place_ref, near_ref, coords_ref, fields_ref, table_ref,
-    out_ref, logdet_ref, cov, weight, sites, sites_t, rhs, swept,
+    out_ref, logdet_ref, cov, weight, sites, sites_t, rhs, panel, swept,
 ):
     tile_index = lax.axis_index("tile")
     wide_index = lax.axis_index("wide")
@@ -152,43 +153,46 @@
         start = pl.multiple_of(r * B, B)
         for p in range(0, B, PANEL):
             rows = [mine[pl.ds(start + p + t, SUB, stride=NB * B), :] for t in range(PANEL)]
-            clean, pivots, back = eliminate(rows, p, lane)
+            pivots, scaled = eliminate(rows, p, lane)
             for t in range(PANEL):
-                weight[pl.ds(p + t, SUB, stride=B), :] = jnp.where(
-                    lane <= p + t, clean[t] * lax.rsqrt(pivots[t]), 0.0)
+                own = jnp.where(lane < p + t, rows[t], jnp.where(lane == p + t, 1.0, 0.0))
+                weight[pl.ds(p + t, SUB, stride=B), :] = own * lax.rsqrt(pivots[t])
                 dets = jnp.where(lane == p + t, pivots[t], dets)
-                swept[pl.ds(t, SUB, stride=PANEL), :] = back[t]
+                panel[pl.ds(t, SUB, stride=PANEL), :] = rows[t]
+                swept[pl.ds(t, SUB, stride=PANEL), :] = scaled[t]
             rest = B - p - PANEL
             if rest == 0:
                 continue
-            ids = lax.broadcasted_iota(jnp.int32, (rest, B), 1)
             for m in range(slots):
-                here = pl.ds(start + m * NB * B + p + PANEL, rest)
-                old = mine[here, :]
-                change = product(left(old), right_cols(swept[m * PANEL : (m + 1) * PANEL, :], p, rest), 0)
-                mine[here, :] = jnp.where((ids >= p) & (ids < p + PANEL), 0.0, old) - change
+                base = start + m * NB * B
+                these = slice(m * PANEL, (m + 1) * PANEL)
+                turned, sweep = swap_sweep(panel[these, :], swept[these, :])
+                change = lax.dot_general(
+                    turned[p + PANEL :], sweep, (((1,), (0,)), ((), ())), preferred_element_type=f32)
+                here = pl.ds(base + p + PANEL, rest)
+                mine[here, :] = mine[here, :] - change
 
         for at in range(NB):
             pl.when(r == at)(lambda at=at: couple(at))
         return dets
 
     def couple(r):
+        later = (NB - 1 - r) * B
         for m in range(slots):
             w = right_rows(weight[m * B : (m + 1) * B, :])
-            solved = product(left(rhs[r, m]), w, 1)
-            rhs[r, m] = solved
-            if r == K:
-                continue
-            later = (NB - 1 - r) * B
-            x = product(left(cov[r, pl.ds((m * NB + r + 1) * B, later), :]), w, 1)
-            x_left = left(x)
-            z_left = left(solved)
+            rhs[r, m] = product(left(rhs[r, m]), w)
+            if r < K:
+                there = pl.ds((m * NB + r + 1) * B, later)
+                cov[r, there, :] = product(left(cov[r, there, :]), w)
+        for m in range(slots if r < K else 0):
+            x = left_short(cov[r, pl.ds((m * NB + r + 1) * B, later), :])
+            z = left_short(rhs[r, m])
             for e in range(r + 1, NB):
                 skip = (e - r - 1) * B
-                y = right_rows(x[skip : skip + B])
+                y = right_short(x[skip : skip + B])
                 here = pl.ds((m * NB + e) * B, later - skip)
-                cov[e, here, :] = cov[e, here, :] - product(tuple(q[skip:] for q in x_left), y, 1)
-                rhs[e, m] = rhs[e, m] - product(z_left, y, 1)
+                cov[e, here, :] = cov[e, here, :] - product_short(x[skip:], y)
+                rhs[e, m] = rhs[e, m] - product_short(z, y)
 
     dets = lax.fori_loop(0, NB, block_step, jnp.ones((SUB, B), f32))
     total = jnp.sum(jnp.log(dets), axis=1, keepdims=True)
@@ -224,6 +228,7 @@
             pltpu.VMEM((B, B), f32),
             pltpu.VMEM((NB, slots, SUB, B), f32),
             pltpu.VMEM((SUB * PANEL, B), f32),
+            pltpu.VMEM((SUB * PANEL, B), f32),
         ],
         compiler_params=pltpu.CompilerParams(vmem_limit_bytes=48 << 20),
     )(counts, place, neighbours, coords, fields, table)

time: 55.1 us -> 47.3 us (0.86)
  Pallas kernels: 36.2 us -> 28.3 us
    pallas_call x1, Pallas kernels: 36.2 us -> 28.3 us  [local(): pl.pallas_call(lambda *refs: whiten_kernel(n_wide, slots, *refs), out_sha...]
where the time goes in v3:
time: 47.3 us; the launch traced here: 47.1 us
  Pallas kernels  28.3 us (60%)
  blocking collectives  9.59 us (20%)
  starting transfers between devices  4.93 us (10%)
  waiting for transfers between devices  1.4 us (3%)
  local copies, waits for them, and re-layouts  1.39 us (3%)
  other arithmetic  0.73 us (2%)
  between operations  0.68 us (1%)
    pallas_call x1, Pallas kernels, local(): pl.pallas_call(lambda *refs: whiten_kernel(n_wide, slots, *refs), out_sha...  28.3 us
    all_gather x1, blocking collectives, local(): table = lax.all_gather(jnp.stack([blocks, prior]), 'wide', axis=0)  9.59 us
    ppermute x1, starting transfers between devices, local(): lax.ppermute(blocks, 'tile', [(i, i + 1) for i in range(n_tile - 1)])  4.93 us
    ppermute x1, waiting for transfers between devices, local(): lax.ppermute(blocks, 'tile', [(i, i + 1) for i in range(n_tile - 1)])  1.4 us
  transfers between devices with their start and end apart: 1, of which 1 were waited for; matrix products, arithmetic and copies ran while one was open for 0% of the time, Pallas kernels for 0%

profile of v3, /device:TPU:0, one launch (start us, length us, event | category | flops | bytes accessed | tf_op | source)
XLA Modules:
  0.0 47.1 jit_solution(17143328693613954720)
XLA Ops:
  0.6 0.0 copy-start.4
  0.6 0.7 %fusion = (f32[1,6,6,128]{3,2,1,0:T(8,128)S(1)}, f32[6,6,128]{2,1,0:T(8,128)S(1)}) fusion(f32[6,4,128]{2,1,0:T(4,128)} %refs_4_.1, f32[6,2,128]{2,1,0:T(2,128)} %refs_3_.1), kind=kLoop, calls=%fused_computation.3 | loop fusion | flops 4608 | bytes 55296 | tf_op jit(solution)/shard_map/stack | solution.py:213
  1.4 4.9 %collective-permute-start = (f32[6,6,128]{2,1,0:T(8,128)S(1)}, f32[6,6,128]{2,1,0:T(8,128)S(1)}, u32[]{:S(2)}, u32[]{:S(2)}) collective-permute-start(f32[6,6,128]{2,1,0:T(8,128)S(1)} %get-tuple-element.7), channel_id=1, source_target_pairs={{0,8},{8,16},{16,24},{1,9},{9,17},{17,25},{2,10},{10,18},{18,26},{... | collective-permute-start | bytes 55304 | tf_op jit(solution)/shard_map/ppermute | solution.py:212
  6.3 0.0 copy-done.4
  6.3 0.1 copy.9.refs_2_
  6.4 1.4 %collective-permute-done = f32[6,6,128]{2,1,0:T(8,128)S(1)} collective-permute-done((f32[6,6,128]{2,1,0:T(8,128)S(1)}, f32[6,6,128]{2,1,0:T(8,128)S(1)}, u32[]{:S(2)}, u32[]{:S(2)}) %collective-permute-start) | collective-permute-done | bytes 18464 | tf_op jit(solution)/shard_map/ppermute | solution.py:212
  7.8 0.0 copy-start
  7.8 0.0 copy-start.1
  7.8 9.6 %all-gather = f32[16,6,6,128]{3,2,1,0:T(8,128)S(1)} all-gather(f32[2,6,6,128]{3,2,1,0:T(8,128)S(1)} %pad_maximum_fusion), channel_id=2, replica_groups=mesh['tile'=4,'wide'=8] {'wide'}, dimensions={0}, use_global_device_ids=true | all-gather | bytes 331776 | tf_op jit(solution)/shard_map/all_gather | solution.py:213
  17.4 0.0 copy-start.2
  17.4 0.0 copy-start.3
  17.4 0.0 copy-done
  17.4 0.0 copy-done.1
  17.4 0.6 %copy-done.2 = s32[1,8]{1,0:T(1,128)S(1)} copy-done((s32[1,8]{1,0:T(1,128)S(1)}, s32[1,8]{1,0:T(1,128)}, u32[]{:S(2)}) %copy-start.2) | copy-done | bytes 56
  18.1 0.0 copy-done.3
  18.1 28.3 %shard_map.68 = (f32[6,4,128]{2,1,0:T(4,128)}, f32[8,128]{1,0:T(8,128)S(1)}) custom-call(s32[1,8]{1,0:T(1,128)S(1)} %copy-done.2, s32[128]{0:T(128)S(1)} %copy-done.3, s32[48,3]{1,0:T(8,128)S(1)} %copy.9.refs_2_, f32[6,2,128]{2,1,0:T(2,128)S(1)} %copy-done.1, f32[6,4,128]{2,1,0:T(4,128)S(1)} %copy-done, f32[8,2,6,6,128]{4,3,2,1,0:T(8,128)S(1)} %bitcast.4), custom_call_target="tpu_custom_call" | custom-call | tf_op jit(solution)/shard_map/pallas_call | solution.py:216
  46.4 0.6 %slice_reduce_fusion = f32[6]{0:T(128)} fusion(f32[8,128]{1,0:T(8,128)S(1)} %get-tuple-element.5), kind=kLoop, calls=%fused_computation.2 | loop fusion | bytes 48 | tf_op jit(solution)/shard_map/slice | solution.py:235
  (1 shorter events, 0.0 us)
Async XLA Ops:
  0.6 5.7 %copy-start.4 = (s32[48,3]{0,1:T(4,128)S(1)}, s32[48,3]{0,1:T(4,128)}, u32[]{:S(2)}) copy-start(s32[48,3]{0,1:T(4,128)} %param.9) | copy-start | bytes 1732
  1.4 6.4 %collective-permute-start = (f32[6,6,128]{2,1,0:T(8,128)S(1)}, f32[6,6,128]{2,1,0:T(8,128)S(1)}, u32[]{:S(2)}, u32[]{:S(2)}) collective-permute-start(f32[6,6,128]{2,1,0:T(8,128)S(1)} %get-tuple-element.7), channel_id=1, source_target_pairs={{0,8},{8,16},{16,24},{1,9},{9,17},{17,25},{2,10},{10,18},{18,26},{... | collective-permute-start | bytes 55304 | tf_op jit(solution)/shard_map/ppermute | solution.py:212
  7.8 9.6 %copy-start = (f32[6,4,128]{2,1,0:T(4,128)S(1)}, f32[6,4,128]{2,1,0:T(4,128)}, u32[]{:S(2)}) copy-start(f32[6,4,128]{2,1,0:T(4,128)} %refs_4_.1) | copy-start | bytes 36868
  7.8 9.6 %copy-start.1 = (f32[6,2,128]{2,1,0:T(2,128)S(1)}, f32[6,2,128]{2,1,0:T(2,128)}, u32[]{:S(2)}) copy-start(f32[6,2,128]{2,1,0:T(2,128)} %refs_3_.1) | copy-start | bytes 18436
  17.4 0.7 %copy-start.2 = (s32[1,8]{1,0:T(1,128)S(1)}, s32[1,8]{1,0:T(1,128)}, u32[]{:S(2)}) copy-start(s32[1,8]{1,0:T(1,128)} %refs_0_.1) | copy-start | bytes 100
  17.4 0.7 %copy-start.3 = (s32[128]{0:T(128)S(1)}, s32[128]{0:T(128)}, u32[]{:S(2)}) copy-start(s32[128]{0:T(128)} %refs_1_.1) | copy-start | bytes 1540

commit v4 on v3

--- a/solution.py
+++ b/solution.py
@@ -13,6 +13,9 @@
 SUB = 8
 PANEL = 16
 GROUP = 8
+LOOK = 1
+TAIL = 1
+DEFER = True
 
 length_scale = 0.08
 nugget = 0.25
@@ -131,74 +134,115 @@
 
     row_id = lax.broadcasted_iota(jnp.int32, (B, B), 0)
     col_id = lax.broadcasted_iota(jnp.int32, (B, B), 1)
-    for m in range(slots):
-        for c in range(NB):
-            at = m * SUB + c
-            x_row = jnp.broadcast_to(sites_t[:, at : at + 1], (B, B))
-            y_row = jnp.broadcast_to(sites_t[:, at + NB : at + NB + 1], (B, B))
-            for r in range(c + 1):
-                dx = x_row - sites[pl.ds(m * SUB + r, 1), :]
-                dy = y_row - sites[pl.ds(m * SUB + NB + r, 1), :]
-                squared = dx * dx + dy * dy
-                scaled = squared * (root_three / length_scale * lax.rsqrt(jnp.maximum(squared, 1e-30)))
-                value = (1.0 + scaled) * jnp.exp(-scaled)
-                if r < K:
-                    value = value * (valid[m, c] * valid[m, r])
-                if c == r:
-                    value = value + jnp.where(row_id == col_id, nugget + 1.0 - valid[m, c], 0.0)
-                cov[r, (m * NB + c) * B : (m * NB + c + 1) * B, :] = value
-
-    def block_step(r, dets):
+
+    def covariance(m, c, columns):
+        at = m * SUB + c
+        x_row = jnp.broadcast_to(sites_t[:, at : at + 1], (B, B))
+        y_row = jnp.broadcast_to(sites_t[:, at + NB : at + NB + 1], (B, B))
+        for r in columns:
+            dx = x_row - sites[pl.ds(m * SUB + r, 1), :]
+            dy = y_row - sites[pl.ds(m * SUB + NB + r, 1), :]
+            squared = dx * dx + dy * dy
+            scaled = squared * (root_three / length_scale * lax.rsqrt(jnp.maximum(squared, 1e-30)))
+            value = (1.0 + scaled) * jnp.exp(-scaled)
+            if r < K:
+                value = value * (valid[m, c] * valid[m, r])
+            if c == r:
+                value = value + jnp.where(row_id == col_id, nugget + 1.0 - valid[m, c], 0.0)
+            cov[r, (m * NB + c) * B : (m * NB + c + 1) * B, :] = value
+
+    for m in range(slots):
+        covariance(m, 0, (0,))
+    later_work = [
+        lambda m=m, c=c: covariance(m, c, range(c + 1)) for c in range(1, NB) for m in range(slots)]
+
+    def factor_block(r):
         mine = cov.at[r]
-        start = pl.multiple_of(r * B, B)
+        rest_of_panel = []
+        pivot_rows = []
         for p in range(0, B, PANEL):
-            rows = [mine[pl.ds(start + p + t, SUB, stride=NB * B), :] for t in range(PANEL)]
+            rows = [mine[pl.ds(r * B + p + t, SUB, stride=NB * B), :] for t in range(PANEL)]
             pivots, scaled = eliminate(rows, p, lane)
+            pivot_rows += pivots
+            for work in rest_of_panel:
+                work()
+            rest_of_panel.clear()
+            for t in range(PANEL):
+                panel[pl.ds(t, SUB, stride=PANEL), :] = rows[t]
+                swept[pl.ds(t, SUB, stride=PANEL), :] = scaled[t]
+            start = p + PANEL
+            if start < B:
+                turns = []
+                for m in range(slots):
+                    these = slice(m * PANEL, (m + 1) * PANEL)
+                    turned, sweep = swap_sweep(panel[these, :], swept[these, :])
+                    turns.append((turned, sweep))
+
+                def update(m, first, last, turned, sweep):
+                    here = pl.ds((m * NB + r) * B + first, last - first)
+                    mine[here, :] = mine[here, :] - lax.dot_general(
+                        turned[first:last], sweep, (((1,), (0,)), ((), ())), preferred_element_type=f32)
+
+                soon = min(B, start + LOOK * PANEL)
+                for m in range(slots):
+                    update(m, start, soon, *turns[m])
+                if soon < B:
+                    rest_of_panel += [
+                        lambda m=m, a=soon, t=turns[m]: update(m, a, B, *t) for m in range(slots)]
             for t in range(PANEL):
                 own = jnp.where(lane < p + t, rows[t], jnp.where(lane == p + t, 1.0, 0.0))
-                weight[pl.ds(p + t, SUB, stride=B), :] = own * lax.rsqrt(pivots[t])
-                dets = jnp.where(lane == p + t, pivots[t], dets)
-                panel[pl.ds(t, SUB, stride=PANEL), :] = rows[t]
-                swept[pl.ds(t, SUB, stride=PANEL), :] = scaled[t]
-            rest = B - p - PANEL
-            if rest == 0:
-                continue
+                weight[r % 2, pl.ds(p + t, SUB, stride=B), :] = own * lax.rsqrt(pivots[t])
+            for _ in range(-(-len(later_work) // max(1, (B - p) // PANEL - TAIL))):
+                later_work.pop(0)()
+        return pivot_rows
+
+    def solve(r, m, c, count):
+        w = right_rows(weight[r % 2, m * B : (m + 1) * B, :])
+        there = pl.ds((m * NB + c) * B, count * B)
+        cov[r, there, :] = product(left(cov[r, there, :]), w)
+
+    def update_block(r, m, c, count, e):
+        x = left_short(cov[r, pl.ds((m * NB + c) * B, count * B), :])
+        y = right_short(left_short(cov[r, pl.ds((m * NB + e) * B, B), :]))
+        here = pl.ds((m * NB + c) * B, count * B)
+        cov[e, here, :] = cov[e, here, :] - product_short(x, y)
+
+    def finish_rhs(r, m):
+        w = right_rows(weight[r % 2, m * B : (m + 1) * B, :])
+        solved = product(left(rhs[r, m]), w)
+        rhs[r, m] = solved
+        z = left_short(solved)
+        for e in range(r + 1, NB):
+            y = right_short(left_short(cov[r, pl.ds((m * NB + e) * B, B), :]))
+            rhs[e, m] = rhs[e, m] - product_short(z, y)
+
+    def rest_of_block(r, m):
+        if r + 2 < NB:
+            solve(r, m, r + 2, NB - r - 2)
+            update_block(r, m, r + 2, NB - r - 2, r + 1)
+            for e in range(r + 2, NB):
+                update_block(r, m, e, NB - e, e)
+        finish_rhs(r, m)
+
+    for r in range(NB):
+        pivot_rows = factor_block(r)
+        if r < K:
             for m in range(slots):
-                base = start + m * NB * B
-                these = slice(m * PANEL, (m + 1) * PANEL)
-                turned, sweep = swap_sweep(panel[these, :], swept[these, :])
-                change = lax.dot_general(
-                    turned[p + PANEL :], sweep, (((1,), (0,)), ((), ())), preferred_element_type=f32)
-                here = pl.ds(base + p + PANEL, rest)
-                mine[here, :] = mine[here, :] - change
-
-        for at in range(NB):
-            pl.when(r == at)(lambda at=at: couple(at))
-        return dets
-
-    def couple(r):
-        later = (NB - 1 - r) * B
-        for m in range(slots):
-            w = right_rows(weight[m * B : (m + 1) * B, :])
-            rhs[r, m] = product(left(rhs[r, m]), w)
-            if r < K:
-                there = pl.ds((m * NB + r + 1) * B, later)
-                cov[r, there, :] = product(left(cov[r, there, :]), w)
-        for m in range(slots if r < K else 0):
-            x = left_short(cov[r, pl.ds((m * NB + r + 1) * B, later), :])
-            z = left_short(rhs[r, m])
-            for e in range(r + 1, NB):
-                skip = (e - r - 1) * B
-                y = right_short(x[skip : skip + B])
-                here = pl.ds((m * NB + e) * B, later - skip)
-                cov[e, here, :] = cov[e, here, :] - product_short(x[skip:], y)
-                rhs[e, m] = rhs[e, m] - product_short(z, y)
-
-    dets = lax.fori_loop(0, NB, block_step, jnp.ones((SUB, B), f32))
+                solve(r, m, r + 1, 1)
+            for m in range(slots):
+                update_block(r, m, r + 1, 1, r + 1)
+        later_work += [lambda r=r, m=m: rest_of_block(r, m) for m in range(slots)]
+        if not DEFER or r == K:
+            for work in later_work:
+                work()
+            later_work.clear()
+    dets = pivot_rows[0]
+    for t in range(1, B):
+        dets = jnp.where(lane == t, pivot_rows[t], dets)
     total = jnp.sum(jnp.log(dets), axis=1, keepdims=True)
     live_count = counts_ref[0, wide_index]
-    slot_id = lax.broadcasted_iota(jnp.int32, (SUB, 1), 0)
-    logdet_ref[...] = jnp.broadcast_to(jnp.where(slot_id < live_count, total, 0.0), (SUB, B))
+    for m in range(slots):
+        logdet_ref[m] = jnp.where(m < live_count, total[m, 0], 0.0)
     for m in range(slots):
         live = (m < live_count).astype(f32)
         out_ref[m] = rhs[K, m, 0:4, :] * live
@@ -213,17 +257,17 @@
     table = lax.all_gather(jnp.stack([blocks, prior]), "wide", axis=0)
     smem = pl.BlockSpec(memory_space=pltpu.SMEM)
     vmem = pl.BlockSpec(memory_space=pltpu.VMEM)
-    result, logs = pl.pallas_call(
+    return pl.pallas_call(
         lambda *refs: whiten_kernel(n_wide, slots, *refs),
         out_shape=(
             jax.ShapeDtypeStruct((slots, 4, B), f32),
-            jax.ShapeDtypeStruct((SUB, B), f32),
+            jax.ShapeDtypeStruct((slots,), f32),
         ),
         in_specs=[smem, smem, smem, vmem, vmem, vmem],
-        out_specs=(vmem, vmem),
+        out_specs=(vmem, smem),
         scratch_shapes=[
             pltpu.VMEM((NB, SUB * NB * B, B), f32),
-            pltpu.VMEM((SUB * B, B), f32),
+            pltpu.VMEM((2, SUB * B, B), f32),
             pltpu.VMEM((B, B), f32),
             pltpu.VMEM((B, B), f32),
             pltpu.VMEM((NB, slots, SUB, B), f32),
@@ -232,7 +276,6 @@
         ],
         compiler_params=pltpu.CompilerParams(vmem_limit_bytes=48 << 20),
     )(counts, place, neighbours, coords, fields, table)
-    return result, logs[:slots, 0]
 
 
 def solution(mesh):

time: 47.3 us -> 42.4 us (0.90)
  Pallas kernels: 28.3 us -> 23.9 us
  local copies, waits for them, and re-layouts: 1.39 us -> 0.77 us
    pallas_call x1, Pallas kernels: 28.3 us -> 23.9 us  [local(): pl.pallas_call(lambda *refs: whiten_kernel(n_wide, slots, *refs), out_sha...]
    slice x1 -> x0, local copies, waits for them, and re-layouts: 0.63 us -> none  [local(): return (result, logs[:slots, 0])]
where the time goes in v4:
time: 42.4 us; the launch traced here: 42.2 us
  Pallas kernels  23.9 us (56%)
  blocking collectives  9.59 us (23%)
  starting transfers between devices  4.93 us (12%)
  waiting for transfers between devices  1.4 us (3%)
  between operations  0.84 us (2%)
  local copies, waits for them, and re-layouts  0.77 us (2%)
  other arithmetic  0.73 us (2%)
    pallas_call x1, Pallas kernels, local(): pl.pallas_call(lambda *refs: whiten_kernel(n_wide, slots, *refs), out_sha...  23.9 us
    all_gather x1, blocking collectives, local(): table = lax.all_gather(jnp.stack([blocks, prior]), 'wide', axis=0)  9.59 us
    ppermute x1, starting transfers between devices, local(): lax.ppermute(blocks, 'tile', [(i, i + 1) for i in range(n_tile - 1)])  4.93 us
    ppermute x1, waiting for transfers between devices, local(): lax.ppermute(blocks, 'tile', [(i, i + 1) for i in range(n_tile - 1)])  1.4 us
  transfers between devices with their start and end apart: 1, of which 1 were waited for; matrix products, arithmetic and copies ran while one was open for 0% of the time, Pallas kernels for 0%

profile of v4, /device:TPU:0, one launch (start us, length us, event | category | flops | bytes accessed | tf_op | source)
XLA Modules:
  0.0 42.2 jit_solution(13398103410198118259)
XLA Ops:
  0.6 0.0 copy-start.4
  0.6 0.7 %fusion = (f32[1,6,6,128]{3,2,1,0:T(8,128)S(1)}, f32[6,6,128]{2,1,0:T(8,128)S(1)}) fusion(f32[6,4,128]{2,1,0:T(4,128)} %refs_4_.1, f32[6,2,128]{2,1,0:T(2,128)} %refs_3_.1), kind=kLoop, calls=%fused_computation.2 | loop fusion | flops 4608 | bytes 55296 | tf_op jit(solution)/shard_map/stack | solution.py:257
  1.4 4.9 %collective-permute-start = (f32[6,6,128]{2,1,0:T(8,128)S(1)}, f32[6,6,128]{2,1,0:T(8,128)S(1)}, u32[]{:S(2)}, u32[]{:S(2)}) collective-permute-start(f32[6,6,128]{2,1,0:T(8,128)S(1)} %get-tuple-element.3), channel_id=1, source_target_pairs={{0,8},{8,16},{16,24},{1,9},{9,17},{17,25},{2,10},{10,18},{18,26},{... | collective-permute-start | bytes 55304 | tf_op jit(solution)/shard_map/ppermute | solution.py:256
  6.3 0.0 copy-done.4
  6.3 0.1 copy.8.refs_2_
  6.4 1.4 %collective-permute-done = f32[6,6,128]{2,1,0:T(8,128)S(1)} collective-permute-done((f32[6,6,128]{2,1,0:T(8,128)S(1)}, f32[6,6,128]{2,1,0:T(8,128)S(1)}, u32[]{:S(2)}, u32[]{:S(2)}) %collective-permute-start) | collective-permute-done | bytes 18464 | tf_op jit(solution)/shard_map/ppermute | solution.py:256
  7.8 0.0 copy-start
  7.8 0.0 copy-start.1
  7.8 9.6 %all-gather = f32[16,6,6,128]{3,2,1,0:T(8,128)S(1)} all-gather(f32[2,6,6,128]{3,2,1,0:T(8,128)S(1)} %pad_maximum_fusion), channel_id=2, replica_groups=mesh['tile'=4,'wide'=8] {'wide'}, dimensions={0}, use_global_device_ids=true | all-gather | bytes 331776 | tf_op jit(solution)/shard_map/all_gather | solution.py:257
  17.4 0.0 copy-start.2
  17.4 0.0 copy-start.3
  17.4 0.0 copy-done
  17.4 0.0 copy-done.1
  17.4 0.6 %copy-done.2 = s32[1,8]{1,0:T(1,128)S(1)} copy-done((s32[1,8]{1,0:T(1,128)S(1)}, s32[1,8]{1,0:T(1,128)}, u32[]{:S(2)}) %copy-start.2) | copy-done | bytes 56
  18.1 0.0 copy-done.3
  18.1 23.9 %shard_map.68 = (f32[6,4,128]{2,1,0:T(4,128)}, f32[6]{0:T(128)}) custom-call(s32[1,8]{1,0:T(1,128)S(1)} %copy-done.2, s32[128]{0:T(128)S(1)} %copy-done.3, s32[48,3]{1,0:T(8,128)S(1)} %copy.8.refs_2_, f32[6,2,128]{2,1,0:T(2,128)S(1)} %copy-done.1, f32[6,4,128]{2,1,0:T(4,128)S(1)} %copy-done, f32[8,2,6,6,128]{4,3,2,1,0:T(8,128)S(1)} %bitcast.4), custom_call_target="tpu_custom_call" | custom-call | tf_op jit(solution)/shard_map/pallas_call | solution.py:260
  (1 shorter events, 0.0 us)
Async XLA Ops:
  0.6 5.7 %copy-start.4 = (s32[48,3]{0,1:T(4,128)S(1)}, s32[48,3]{0,1:T(4,128)}, u32[]{:S(2)}) copy-start(s32[48,3]{0,1:T(4,128)} %param.9) | copy-start | bytes 1732
  1.4 6.4 %collective-permute-start = (f32[6,6,128]{2,1,0:T(8,128)S(1)}, f32[6,6,128]{2,1,0:T(8,128)S(1)}, u32[]{:S(2)}, u32[]{:S(2)}) collective-permute-start(f32[6,6,128]{2,1,0:T(8,128)S(1)} %get-tuple-element.3), channel_id=1, source_target_pairs={{0,8},{8,16},{16,24},{1,9},{9,17},{17,25},{2,10},{10,18},{18,26},{... | collective-permute-start | bytes 55304 | tf_op jit(solution)/shard_map/ppermute | solution.py:256
  7.8 9.6 %copy-start = (f32[6,4,128]{2,1,0:T(4,128)S(1)}, f32[6,4,128]{2,1,0:T(4,128)}, u32[]{:S(2)}) copy-start(f32[6,4,128]{2,1,0:T(4,128)} %refs_4_.1) | copy-start | bytes 36868
  7.8 9.6 %copy-start.1 = (f32[6,2,128]{2,1,0:T(2,128)S(1)}, f32[6,2,128]{2,1,0:T(2,128)}, u32[]{:S(2)}) copy-start(f32[6,2,128]{2,1,0:T(2,128)} %refs_3_.1) | copy-start | bytes 18436
  17.4 0.7 %copy-start.2 = (s32[1,8]{1,0:T(1,128)S(1)}, s32[1,8]{1,0:T(1,128)}, u32[]{:S(2)}) copy-start(s32[1,8]{1,0:T(1,128)} %refs_0_.1) | copy-start | bytes 100
  17.4 0.7 %copy-start.3 = (s32[128]{0:T(128)S(1)}, s32[128]{0:T(128)}, u32[]{:S(2)}) copy-start(s32[128]{0:T(128)} %refs_1_.1) | copy-start | bytes 1540

commit v5 on v4

--- a/solution.py
+++ b/solution.py
@@ -13,6 +13,9 @@
 SUB = 8
 PANEL = 16
 GROUP = 8
+COV = NB * B + 8
+FACTOR = B + 8
+SWEEP = PANEL + 8
 LOOK = 1
 TAIL = 1
 DEFER = True
@@ -89,23 +92,33 @@
         for s in range(g, end):
             for i in range(s, n):
                 cols[i, s] = column(rows[i], first + s)
-        for t in range(g, end):
+        for t in range(g, end, 2):
+            v = t + 1
             pivot = cols[t, t]
+            cross = cols[v, t]
             inv = 1.0 / pivot
-            pivots.append(pivot)
-            scaled.append(jnp.where(lane == first + t, 1.0 + pivot, rows[t]) * inv)
-            for u in range(t + 1, end):
-                lower = cols[u, t] * inv
+            both = pivot * cols[v, v] - cross * cross
+            inv_next = pivot * (1.0 / both)
+            lower = cross * inv
+            next_pivot = cols[v, v] - cross * lower
+            pivots += [pivot, next_pivot]
+            head = jnp.where(lane == first + t, 1.0 + pivot, rows[t]) * inv
+            rows[v] = rows[v] - cross * head
+            tail = jnp.where(lane == first + v, 1.0 + next_pivot, rows[v]) * inv_next
+            scaled += [head, tail]
+            after = {i: cols[i, v] - cols[i, t] * lower for i in range(v + 1, n)}
+            for u in range(v + 1, end):
+                one = cols[u, t] * inv
+                two = after[u] * inv_next
                 for i in range(u, n):
-                    cols[i, u] = cols[i, u] - cols[i, t] * lower
-                rows[u] = rows[u] - cols[u, t] * scaled[t]
-            for i in range(end, n):
-                rows[i] = rows[i] - cols[i, t] * scaled[t]
+                    cols[i, u] = cols[i, u] - cols[i, t] * one - after[i] * two
+            for i in range(v + 1, n):
+                rows[i] = rows[i] - cols[i, t] * head - after[i] * tail
     return pivots, scaled
 
 
 def whiten_kernel(
-    n_wide, slots, counts_ref, place_ref, near_ref, coords_ref, fields_ref, table_ref,
+    n_wide, slots, n_place, meta_ref, table_ref,
     out_ref, logdet_ref, cov, weight, sites, sites_t, rhs, panel, swept,
 ):
     tile_index = lax.axis_index("tile")
@@ -117,18 +130,20 @@
     valid = {}
     for m in range(slots):
         for k in range(K):
-            listed = near_ref[wide_index * slots + m, k]
+            listed = meta_ref[n_wide + n_place + (wide_index * slots + m) * K + k]
             valid[m, k] = (listed >= 0).astype(f32)
-            source = place_ref[jnp.maximum(listed, 0)]
+            source = meta_ref[n_wide + jnp.maximum(listed, 0)]
             device = source // slots
-            prior = (device // n_wide != tile_index).astype(jnp.int32)
-            block = table_ref[device % n_wide, prior, source % slots]
+            tile = device // n_wide
+            prior = (tile != tile_index).astype(jnp.int32)
+            block = table_ref[device - tile * n_wide, prior, source - device * slots]
             sites[pl.ds(m * SUB + k, 1), :] = block[0:1]
             sites[pl.ds(m * SUB + NB + k, 1), :] = block[1:2]
             rhs[k, m, 0:4, :] = block[2:6] * valid[m, k]
-        sites[pl.ds(m * SUB + K, 1), :] = coords_ref[m, 0:1, :]
-        sites[pl.ds(m * SUB + NB + K, 1), :] = coords_ref[m, 1:2, :]
-        rhs[K, m, 0:4, :] = fields_ref[m]
+        block = table_ref[wide_index, 0, m]
+        sites[pl.ds(m * SUB + K, 1), :] = block[0:1]
+        sites[pl.ds(m * SUB + NB + K, 1), :] = block[1:2]
+        rhs[K, m, 0:4, :] = block[2:6]
         valid[m, K] = 1.0
     sites_t[...] = sites[...].T
 
@@ -149,7 +164,7 @@
                 value = value * (valid[m, c] * valid[m, r])
             if c == r:
                 value = value + jnp.where(row_id == col_id, nugget + 1.0 - valid[m, c], 0.0)
-            cov[r, (m * NB + c) * B : (m * NB + c + 1) * B, :] = value
+            cov[r, m * COV + c * B : m * COV + (c + 1) * B, :] = value
 
     for m in range(slots):
         covariance(m, 0, (0,))
@@ -161,25 +176,25 @@
         rest_of_panel = []
         pivot_rows = []
         for p in range(0, B, PANEL):
-            rows = [mine[pl.ds(r * B + p + t, SUB, stride=NB * B), :] for t in range(PANEL)]
+            rows = [mine[pl.ds(r * B + p + t, SUB, stride=COV), :] for t in range(PANEL)]
             pivots, scaled = eliminate(rows, p, lane)
             pivot_rows += pivots
             for work in rest_of_panel:
                 work()
             rest_of_panel.clear()
             for t in range(PANEL):
-                panel[pl.ds(t, SUB, stride=PANEL), :] = rows[t]
-                swept[pl.ds(t, SUB, stride=PANEL), :] = scaled[t]
+                panel[pl.ds(t, SUB, stride=SWEEP), :] = rows[t]
+                swept[pl.ds(t, SUB, stride=SWEEP), :] = scaled[t]
             start = p + PANEL
             if start < B:
                 turns = []
                 for m in range(slots):
-                    these = slice(m * PANEL, (m + 1) * PANEL)
+                    these = slice(m * SWEEP, m * SWEEP + PANEL)
                     turned, sweep = swap_sweep(panel[these, :], swept[these, :])
                     turns.append((turned, sweep))
 
                 def update(m, first, last, turned, sweep):
-                    here = pl.ds((m * NB + r) * B + first, last - first)
+                    here = pl.ds(m * COV + r * B + first, last - first)
                     mine[here, :] = mine[here, :] - lax.dot_general(
                         turned[first:last], sweep, (((1,), (0,)), ((), ())), preferred_element_type=f32)
 
@@ -191,29 +206,29 @@
                         lambda m=m, a=soon, t=turns[m]: update(m, a, B, *t) for m in range(slots)]
             for t in range(PANEL):
                 own = jnp.where(lane < p + t, rows[t], jnp.where(lane == p + t, 1.0, 0.0))
-                weight[r % 2, pl.ds(p + t, SUB, stride=B), :] = own * lax.rsqrt(pivots[t])
+                weight[r % 2, pl.ds(p + t, SUB, stride=FACTOR), :] = own * lax.rsqrt(pivots[t])
             for _ in range(-(-len(later_work) // max(1, (B - p) // PANEL - TAIL))):
                 later_work.pop(0)()
         return pivot_rows
 
     def solve(r, m, c, count):
-        w = right_rows(weight[r % 2, m * B : (m + 1) * B, :])
-        there = pl.ds((m * NB + c) * B, count * B)
+        w = right_rows(weight[r % 2, m * FACTOR : m * FACTOR + B, :])
+        there = pl.ds(m * COV + c * B, count * B)
         cov[r, there, :] = product(left(cov[r, there, :]), w)
 
     def update_block(r, m, c, count, e):
-        x = left_short(cov[r, pl.ds((m * NB + c) * B, count * B), :])
-        y = right_short(left_short(cov[r, pl.ds((m * NB + e) * B, B), :]))
-        here = pl.ds((m * NB + c) * B, count * B)
+        x = left_short(cov[r, pl.ds(m * COV + c * B, count * B), :])
+        y = right_short(left_short(cov[r, pl.ds(m * COV + e * B, B), :]))
+        here = pl.ds(m * COV + c * B, count * B)
         cov[e, here, :] = cov[e, here, :] - product_short(x, y)
 
     def finish_rhs(r, m):
-        w = right_rows(weight[r % 2, m * B : (m + 1) * B, :])
+        w = right_rows(weight[r % 2, m * FACTOR : m * FACTOR + B, :])
         solved = product(left(rhs[r, m]), w)
         rhs[r, m] = solved
         z = left_short(solved)
         for e in range(r + 1, NB):
-            y = right_short(left_short(cov[r, pl.ds((m * NB + e) * B, B), :]))
+            y = right_short(left_short(cov[r, pl.ds(m * COV + e * B, B), :]))
             rhs[e, m] = rhs[e, m] - product_short(z, y)
 
     def rest_of_block(r, m):
@@ -240,7 +255,7 @@
     for t in range(1, B):
         dets = jnp.where(lane == t, pivot_rows[t], dets)
     total = jnp.sum(jnp.log(dets), axis=1, keepdims=True)
-    live_count = counts_ref[0, wide_index]
+    live_count = meta_ref[wide_index]
     for m in range(slots):
         logdet_ref[m] = jnp.where(m < live_count, total[m, 0], 0.0)
     for m in range(slots):
@@ -255,27 +270,28 @@
     blocks = jnp.concatenate([coords, fields], axis=1)
     prior = lax.ppermute(blocks, "tile", [(i, i + 1) for i in range(n_tile - 1)])
     table = lax.all_gather(jnp.stack([blocks, prior]), "wide", axis=0)
+    meta = jnp.concatenate([counts.reshape(-1), place, neighbours.reshape(-1)])
     smem = pl.BlockSpec(memory_space=pltpu.SMEM)
     vmem = pl.BlockSpec(memory_space=pltpu.VMEM)
     return pl.pallas_call(
-        lambda *refs: whiten_kernel(n_wide, slots, *refs),
+        lambda *refs: whiten_kernel(n_wide, slots, place.shape[0], *refs),
         out_shape=(
             jax.ShapeDtypeStruct((slots, 4, B), f32),
             jax.ShapeDtypeStruct((slots,), f32),
         ),
-        in_specs=[smem, smem, smem, vmem, vmem, vmem],
+        in_specs=[smem, vmem],
         out_specs=(vmem, smem),
         scratch_shapes=[
-            pltpu.VMEM((NB, SUB * NB * B, B), f32),
-            pltpu.VMEM((2, SUB * B, B), f32),
+            pltpu.VMEM((NB, (SUB + 1) * COV, B), f32),
+            pltpu.VMEM((2, (SUB + 1) * FACTOR, B), f32),
             pltpu.VMEM((B, B), f32),
             pltpu.VMEM((B, B), f32),
             pltpu.VMEM((NB, slots, SUB, B), f32),
-            pltpu.VMEM((SUB * PANEL, B), f32),
-            pltpu.VMEM((SUB * PANEL, B), f32),
+            pltpu.VMEM(((SUB + 1) * SWEEP, B), f32),
+            pltpu.VMEM(((SUB + 1) * SWEEP, B), f32),
         ],
         compiler_params=pltpu.CompilerParams(vmem_limit_bytes=48 << 20),
-    )(counts, place, neighbours, coords, fields, table)
+    )(meta, table)
 
 
 def solution(mesh):

time: 42.4 us -> 40.6 us (0.958)
  Pallas kernels: 23.9 us -> 22.8 us
  waiting for transfers between devices: 1.4 us -> 0.52 us
    pallas_call x1, Pallas kernels: 23.9 us -> 22.8 us  [local(): pl.pallas_call(lambda *refs: whiten_kernel(n_wide, slots, place.shape[0],...]
    ppermute x1, waiting for transfers between devices: 1.4 us -> 0.52 us  [local(): lax.ppermute(blocks, 'tile', [(i, i + 1) for i in range(n_tile - 1)])]
  transfers between devices with their start and end apart: 1 -> 1, of which waited for: 1 -> 1; matrix products, arithmetic and copies ran while one was open for 0% -> 1% of each run, Pallas kernels for 0% -> 0%
where the time goes in v5:
time: 40.6 us; the launch traced here: 40.3 us
  Pallas kernels  22.8 us (56%)
  blocking collectives  9.58 us (24%)
  starting transfers between devices  4.93 us (12%)
  local copies, waits for them, and re-layouts  0.88 us (2%)
  between operations  0.84 us (2%)
  other arithmetic  0.81 us (2%)
  waiting for transfers between devices  0.52 us (1%)
    pallas_call x1, Pallas kernels, local(): pl.pallas_call(lambda *refs: whiten_kernel(n_wide, slots, place.shape[0],...  22.8 us
    all_gather x1, blocking collectives, local(): table = lax.all_gather(jnp.stack([blocks, prior]), 'wide', axis=0)  9.58 us
    ppermute x1, starting transfers between devices, local(): lax.ppermute(blocks, 'tile', [(i, i + 1) for i in range(n_tile - 1)])  4.93 us
  transfers between devices with their start and end apart: 1, of which 1 were waited for; matrix products, arithmetic and copies ran while one was open for 1% of the time, Pallas kernels for 0%

profile of v5, /device:TPU:0, one launch (start us, length us, event | category | flops | bytes accessed | tf_op | source)
XLA Modules:
  0.0 40.3 jit_solution(18308780518217300379)
XLA Ops:
  0.6 0.0 copy-start
  0.6 0.7 %fusion = (f32[1,6,6,128]{3,2,1,0:T(8,128)S(1)}, f32[6,6,128]{2,1,0:T(8,128)S(1)}) fusion(f32[6,4,128]{2,1,0:T(4,128)} %param.6, f32[6,2,128]{2,1,0:T(2,128)} %param.5), kind=kLoop, calls=%fused_computation.3 | loop fusion | flops 4608 | bytes 55296 | tf_op jit(solution)/shard_map/stack | solution.py:272
  1.4 4.9 %collective-permute-start = (f32[6,6,128]{2,1,0:T(8,128)S(1)}, f32[6,6,128]{2,1,0:T(8,128)S(1)}, u32[]{:S(2)}, u32[]{:S(2)}) collective-permute-start(f32[6,6,128]{2,1,0:T(8,128)S(1)} %get-tuple-element.3), channel_id=1, source_target_pairs={{0,8},{8,16},{16,24},{1,9},{9,17},{17,25},{2,10},{10,18},{18,26},{... | collective-permute-start | bytes 55304 | tf_op jit(solution)/shard_map/ppermute | solution.py:271
  6.3 0.0 copy-done
  6.3 0.1 copy.8
  6.4 0.1 reshape.11
  6.5 0.0 copy-start.1
  6.5 0.0 copy-start.2
  6.6 0.6 %copy-done.1 = s32[128]{0:T(128)S(1)} copy-done((s32[128]{0:T(128)S(1)}, s32[128]{0:T(128)}, u32[]{:S(2)}) %copy-start.1) | copy-done | bytes 536
  7.2 0.0 copy-done.2
  7.2 0.1 pad_add_fusion.refs_0_
  7.3 0.5 %collective-permute-done = f32[6,6,128]{2,1,0:T(8,128)S(1)} collective-permute-done((f32[6,6,128]{2,1,0:T(8,128)S(1)}, f32[6,6,128]{2,1,0:T(8,128)S(1)}, u32[]{:S(2)}, u32[]{:S(2)}) %collective-permute-start) | collective-permute-done | bytes 18464 | tf_op jit(solution)/shard_map/ppermute | solution.py:271
  7.8 9.6 %all-gather = f32[16,6,6,128]{3,2,1,0:T(8,128)S(1)} all-gather(f32[2,6,6,128]{3,2,1,0:T(8,128)S(1)} %pad_maximum_fusion), channel_id=2, replica_groups=mesh['tile'=4,'wide'=8] {'wide'}, dimensions={0}, use_global_device_ids=true | all-gather | bytes 331776 | tf_op jit(solution)/shard_map/all_gather | solution.py:272
  17.4 22.8 %shard_map.68 = (f32[6,4,128]{2,1,0:T(4,128)}, f32[6]{0:T(128)}) custom-call(s32[280]{0:T(512)S(1)} %pad_add_fusion.refs_0_, f32[8,2,6,6,128]{4,3,2,1,0:T(8,128)S(1)} %bitcast.5), custom_call_target="tpu_custom_call" | custom-call | tf_op jit(solution)/shard_map/pallas_call | solution.py:276
  (1 shorter events, 0.0 us)
Async XLA Ops:
  0.6 5.7 %copy-start = (s32[48,3]{0,1:T(4,128)S(1)}, s32[48,3]{0,1:T(4,128)}, u32[]{:S(2)}) copy-start(s32[48,3]{0,1:T(4,128)} %param.9) | copy-start | bytes 1732
  1.4 6.4 %collective-permute-start = (f32[6,6,128]{2,1,0:T(8,128)S(1)}, f32[6,6,128]{2,1,0:T(8,128)S(1)}, u32[]{:S(2)}, u32[]{:S(2)}) collective-permute-start(f32[6,6,128]{2,1,0:T(8,128)S(1)} %get-tuple-element.3), channel_id=1, source_target_pairs={{0,8},{8,16},{16,24},{1,9},{9,17},{17,25},{2,10},{10,18},{18,26},{... | collective-permute-start | bytes 55304 | tf_op jit(solution)/shard_map/ppermute | solution.py:271
  6.5 0.7 %copy-start.1 = (s32[128]{0:T(128)S(1)}, s32[128]{0:T(128)}, u32[]{:S(2)}) copy-start(s32[128]{0:T(128)} %param.8) | copy-start | bytes 1540
  6.5 0.7 %copy-start.2 = (s32[1,8]{1,0:T(1,128)S(1)}, s32[1,8]{1,0:T(1,128)}, u32[]{:S(2)}) copy-start(s32[1,8]{1,0:T(1,128)} %param.7) | copy-start | bytes 100

commit v6 on v5

--- a/solution.py
+++ b/solution.py
@@ -214,7 +214,9 @@
     def solve(r, m, c, count):
         w = right_rows(weight[r % 2, m * FACTOR : m * FACTOR + B, :])
         there = pl.ds(m * COV + c * B, count * B)
-        cov[r, there, :] = product(left(cov[r, there, :]), w)
+        x = product(left(cov[r, there, :]), w)
+        cov[r, there, :] = x
+        return x
 
     def update_block(r, m, c, count, e):
         x = left_short(cov[r, pl.ds(m * COV + c * B, count * B), :])
@@ -242,10 +244,11 @@
     for r in range(NB):
         pivot_rows = factor_block(r)
         if r < K:
+            solved = [solve(r, m, r + 1, 1) for m in range(slots)]
             for m in range(slots):
-                solve(r, m, r + 1, 1)
-            for m in range(slots):
-                update_block(r, m, r + 1, 1, r + 1)
+                x = left_short(solved[m])
+                here = pl.ds(m * COV + (r + 1) * B, B)
+                cov[r + 1, here, :] = cov[r + 1, here, :] - product_short(x, right_short(x))
         later_work += [lambda r=r, m=m: rest_of_block(r, m) for m in range(slots)]
         if not DEFER or r == K:
             for work in later_work:

time: 40.6 us -> 40.6 us (level)
  no operation moved by 1% of the time
where the time goes in v6:
time: 40.6 us; the launch traced here: 40.4 us
  Pallas kernels  22.8 us (56%)
  blocking collectives  9.58 us (24%)
  starting transfers between devices  4.93 us (12%)
  local copies, waits for them, and re-layouts  0.88 us (2%)
  between operations  0.84 us (2%)
  other arithmetic  0.81 us (2%)
  waiting for transfers between devices  0.52 us (1%)
    pallas_call x1, Pallas kernels, local(): pl.pallas_call(lambda *refs: whiten_kernel(n_wide, slots, place.shape[0],...  22.8 us
    all_gather x1, blocking collectives, local(): table = lax.all_gather(jnp.stack([blocks, prior]), 'wide', axis=0)  9.58 us
    ppermute x1, starting transfers between devices, local(): lax.ppermute(blocks, 'tile', [(i, i + 1) for i in range(n_tile - 1)])  4.93 us
  transfers between devices with their start and end apart: 1, of which 1 were waited for; matrix products, arithmetic and copies ran while one was open for 1% of the time, Pallas kernels for 0%

profile of v6, /device:TPU:0, one launch (start us, length us, event | category | flops | bytes accessed | tf_op | source)
XLA Modules:
  0.0 40.4 jit_solution(5491172620150955274)
XLA Ops:
  0.6 0.0 copy-start
  0.6 0.7 %fusion = (f32[1,6,6,128]{3,2,1,0:T(8,128)S(1)}, f32[6,6,128]{2,1,0:T(8,128)S(1)}) fusion(f32[6,4,128]{2,1,0:T(4,128)} %param.6, f32[6,2,128]{2,1,0:T(2,128)} %param.5), kind=kLoop, calls=%fused_computation.3 | loop fusion | flops 4608 | bytes 55296 | tf_op jit(solution)/shard_map/stack | solution.py:275
  1.4 4.9 %collective-permute-start = (f32[6,6,128]{2,1,0:T(8,128)S(1)}, f32[6,6,128]{2,1,0:T(8,128)S(1)}, u32[]{:S(2)}, u32[]{:S(2)}) collective-permute-start(f32[6,6,128]{2,1,0:T(8,128)S(1)} %get-tuple-element.3), channel_id=1, source_target_pairs={{0,8},{8,16},{16,24},{1,9},{9,17},{17,25},{2,10},{10,18},{18,26},{... | collective-permute-start | bytes 55304 | tf_op jit(solution)/shard_map/ppermute | solution.py:274
  6.3 0.0 copy-done
  6.3 0.1 copy.8
  6.4 0.1 reshape.11
  6.5 0.0 copy-start.1
  6.5 0.0 copy-start.2
  6.6 0.6 %copy-done.1 = s32[128]{0:T(128)S(1)} copy-done((s32[128]{0:T(128)S(1)}, s32[128]{0:T(128)}, u32[]{:S(2)}) %copy-start.1) | copy-done | bytes 536
  7.2 0.0 copy-done.2
  7.2 0.1 pad_add_fusion.refs_0_
  7.3 0.5 %collective-permute-done = f32[6,6,128]{2,1,0:T(8,128)S(1)} collective-permute-done((f32[6,6,128]{2,1,0:T(8,128)S(1)}, f32[6,6,128]{2,1,0:T(8,128)S(1)}, u32[]{:S(2)}, u32[]{:S(2)}) %collective-permute-start) | collective-permute-done | bytes 18464 | tf_op jit(solution)/shard_map/ppermute | solution.py:274
  7.8 9.6 %all-gather = f32[16,6,6,128]{3,2,1,0:T(8,128)S(1)} all-gather(f32[2,6,6,128]{3,2,1,0:T(8,128)S(1)} %pad_maximum_fusion), channel_id=2, replica_groups=mesh['tile'=4,'wide'=8] {'wide'}, dimensions={0}, use_global_device_ids=true | all-gather | bytes 331776 | tf_op jit(solution)/shard_map/all_gather | solution.py:275
  17.4 22.8 %shard_map.68 = (f32[6,4,128]{2,1,0:T(4,128)}, f32[6]{0:T(128)}) custom-call(s32[280]{0:T(512)S(1)} %pad_add_fusion.refs_0_, f32[8,2,6,6,128]{4,3,2,1,0:T(8,128)S(1)} %bitcast.5), custom_call_target="tpu_custom_call" | custom-call | tf_op jit(solution)/shard_map/pallas_call | solution.py:279
  (1 shorter events, 0.0 us)
Async XLA Ops:
  0.6 5.7 %copy-start = (s32[48,3]{0,1:T(4,128)S(1)}, s32[48,3]{0,1:T(4,128)}, u32[]{:S(2)}) copy-start(s32[48,3]{0,1:T(4,128)} %param.9) | copy-start | bytes 1732
  1.4 6.4 %collective-permute-start = (f32[6,6,128]{2,1,0:T(8,128)S(1)}, f32[6,6,128]{2,1,0:T(8,128)S(1)}, u32[]{:S(2)}, u32[]{:S(2)}) collective-permute-start(f32[6,6,128]{2,1,0:T(8,128)S(1)} %get-tuple-element.3), channel_id=1, source_target_pairs={{0,8},{8,16},{16,24},{1,9},{9,17},{17,25},{2,10},{10,18},{18,26},{... | collective-permute-start | bytes 55304 | tf_op jit(solution)/shard_map/ppermute | solution.py:274
  6.5 0.7 %copy-start.1 = (s32[128]{0:T(128)S(1)}, s32[128]{0:T(128)}, u32[]{:S(2)}) copy-start(s32[128]{0:T(128)} %param.8) | copy-start | bytes 1540
  6.5 0.7 %copy-start.2 = (s32[1,8]{1,0:T(1,128)S(1)}, s32[1,8]{1,0:T(1,128)}, u32[]{:S(2)}) copy-start(s32[1,8]{1,0:T(1,128)} %param.7) | copy-start | bytes 100
